TPU v7x, 256 devices: a whole 4x4x8 slice. The times are simulated.
256 devices in a mesh: band: 64 (over z, y, x_lo), slab: 4 (over x_hi, core).
Axes of the slice: x: 4 (x_hi: 2, x_lo: 2; x = x_hi * 2 + x_lo), y: 4, z: 8, core: 2. Of those that a mesh axis runs over, the one named last changes fastest.
Arguments:
- bands: float32 [256, 32, 24, 128], P('band', 'slab'), may hold values from -8 to 8
- potential: float32 [32, 24, 128], P('slab'), may hold values from -1 to 0
Outputs:
- filtered: float32 [256, 32, 24, 128], P('band', 'slab')
- correlation: float32 [256, 256], P('band')
- projected: float32 [256, 256], P('band')
All inputs are finite; a program needn't handle non-finite values.
Results may differ from a plain program's by a relative error of at most 0.000092.
Values sent between devices are 32-bit elements; how exact they have to be, the bound alone decides.
No kernel may reach another device: no remote copies, remote signals or barrier semaphores. Data moves between devices by JAX's collectives and lax.ppermute only.
A program may use at most 128 MiB of HBM per device.

v0:
```python
import jax
import jax.numpy as jnp
from jax import lax
from jax.experimental import pallas as pl
from jax.experimental.pallas import tpu as pltpu
from jax.sharding import Mesh, PartitionSpec as P


centre = 4.5
half = 3.5
scale = 2.0 / half

VMEM = pl.BlockSpec(memory_space=pltpu.VMEM)


def neighbours(v):
    one, two = [], []
    for axis in (0, 1):
        size = v.shape[axis]
        one.append(pltpu.roll(v, 1, axis) + pltpu.roll(v, size - 1, axis))
        two.append(pltpu.roll(v, 2, axis) + pltpu.roll(v, size - 2, axis))
    return one[0] + one[1], two[0] + two[1]


def stencil(at, z):
    v = at(z)
    one, two = neighbours(v)
    one = one + (at(z - 1) + at(z + 1))
    two = two + (at(z - 2) + at(z + 2))
    return v, one, two


def filter_kernel(odd_ref, near_ref, mid_ref, far_ref, ends_ref, pnear_ref, pmid_ref, pfar_ref, *rest):
    odd = odd_ref[0]

    @pl.when(odd == 0)
    def _():
        filter_bands(far_ref, mid_ref, near_ref, ends_ref, pfar_ref, pmid_ref, pnear_ref, *rest)

    @pl.when(odd == 1)
    def _():
        filter_bands(near_ref, mid_ref, far_ref, ends_ref, pnear_ref, pmid_ref, pfar_ref, *rest)


def filter_bands(
    low_ref, mid_ref, high_ref, far_ref, plow_ref, pmid_ref, phigh_ref,
    filt_ref, send_ref,
    a_ref, b_ref, image_ref, weight_ref,
):
    bands, thick = mid_ref.shape[:2]
    edge = far_ref.shape[1] // 2
    total = 3 * thick + 2 * edge
    own = thick + edge

    for part, ref in enumerate((plow_ref, pmid_ref, phigh_ref)):
        for z in range(thick):
            weight_ref[edge + part * thick + z] = (ref[z] + (3.75 - centre)) * scale

    def one_band(band, carry):
        def start(z):
            z = z - edge
            if z < 0:
                return far_ref[band, z + 2 * edge]
            if z >= 3 * thick:
                return far_ref[band, z - 3 * thick]
            return (low_ref, mid_ref, high_ref)[z // thick][band, z % thick]

        def held(ref):
            return lambda z: ref[z]

        def step(at, z):
            v, one, two = stencil(at, z)
            return v, weight_ref[z] * v - (scale * 2.0 / 3.0) * one + (scale / 24.0) * two

        for z in range(2, total - 2):
            a_ref[z] = 0.5 * step(start, z)[1]
        for z in range(4, total - 4):
            b_ref[z] = step(held(a_ref), z)[1] - start(z)
        for z in range(6, total - 6):
            a_ref[z] = step(held(b_ref), z)[1] - a_ref[z]
        for z in range(8, total - 8):
            new = step(held(a_ref), z)[1] - b_ref[z]
            b_ref[z] = new
            if own <= z < own + thick:
                filt_ref[band, z - own] = new
        for z in range(thick):
            v, full = step(held(b_ref), z + own)
            image_ref[z] = (0.5 * half) * full + centre * v
        per = image_ref.shape[1] // 3
        for z in range(thick):
            for f, at in enumerate((filt_ref.at[band, z], image_ref.at[z])):
                for k in range(3):
                    first = ((z * per * bands + band) * 2 + f) * 3 + k
                    send_ref[pl.ds(first, per, stride=6 * bands), :] = at[pl.ds(k, per, stride=3), :]
        return carry

    lax.fori_loop(0, bands, one_band, 0)


def gram_kernel(planes, per_chunk, *refs):
    recv_refs, out_ref, held = refs[:-7], refs[-7], refs[-6:]
    size = held[0].shape[0]
    bands = per_chunk * len(recv_refs)
    groups = size // bands
    across = size // planes
    for f in range(2):
        for k in range(3):
            for band in range(bands):
                ref = recv_refs[band // per_chunk]
                first = ((band % per_chunk) * 2 + f) * 3 + k
                part = ref[pl.ds(first, groups, stride=6 * per_chunk), :]
                held[f * 3 + k][pl.ds(band, groups, stride=bands), :] = part
    filt = jnp.concatenate([ref[...] for ref in held[:3]], axis=1)
    image = jnp.concatenate([ref[...] for ref in held[3:]], axis=1)
    for f, left in enumerate((filt, image)):
        block = lax.dot_general(
            left,
            filt,
            (((1,), (1,)), ((), ())),
            precision=lax.Precision.HIGHEST,
            preferred_element_type=jnp.float32,
        )
        for z in range(planes):
            for c in range(2):
                part = block[z * across : (z + 1) * across, c * 128 : (c + 1) * 128]
                out_ref[pl.ds((z * 2 + f) * 2 + c, across, stride=4 * planes), :] = part


def spread_kernel(recv_ref, out_ref):
    total = jnp.sum(recv_ref[...], axis=0)
    planes = total.shape[0] // 4
    for z in range(planes):
        for s in range(4):
            out_ref[z * 4 + s] = total[z * 4 : (z + 1) * 4]


def finish_kernel(volume, recv_ref, corr_ref, proj_ref):
    total = jnp.sum(recv_ref[...], axis=0) * volume
    for s in range(4):
        for c in range(2):
            lanes = slice(c * 128, (c + 1) * 128)
            corr_ref[s : s + 1, lanes] = total[s * 4 + c : s * 4 + c + 1]
            proj_ref[s : s + 1, lanes] = total[s * 4 + 2 + c : s * 4 + 3 + c]


def shape(*dims):
    return jax.ShapeDtypeStruct(dims, jnp.float32)


def call(kernel, outs, scratch=(), scalars=0):
    one = not isinstance(outs, tuple)

    def run(*args):
        return pl.pallas_call(
            kernel,
            out_shape=outs,
            in_specs=[pl.BlockSpec(memory_space=pltpu.SMEM)] * scalars + [VMEM] * (len(args) - scalars),
            out_specs=VMEM if one else (VMEM,) * len(outs),
            scratch_shapes=[pltpu.VMEM(dims, jnp.float32) for dims in scratch],
            compiler_params=pltpu.CompilerParams(vmem_limit_bytes=16 * 2**20),
        )(*args)

    return run


CHUNKS = 1


def work(bands, potential):
    slabs = lax.axis_size("slab")
    planes = lax.axis_size("z")
    across = lax.axis_size("y") * lax.axis_size("x") * slabs
    groups = planes * across // slabs
    count, thick, ny, nx = bands.shape
    near = [(0, 1), (1, 0), (2, 3), (3, 2)]
    far = [(0, 3), (3, 0), (1, 2), (2, 1)]
    odd = jnp.reshape(lax.axis_index("slab") % 2, (1,)).astype(jnp.int32)
    each = count // CHUNKS
    rows = each * 2 * thick * ny

    pieces = []
    for chunk in range(CHUNKS):
        mid = bands[chunk * each : (chunk + 1) * each]
        other = lax.ppermute(mid, "slab", far)
        beside = lax.ppermute(mid, "slab", near)
        ends = jnp.concatenate([other[:, :2], other[:, -2:]], axis=1)
        ends = lax.ppermute(ends, "slab", near)
        pieces.append((beside, mid, other, ends))
    pfar = lax.ppermute(potential, "slab", far)
    pnear = lax.ppermute(potential, "slab", near)

    filtered, received = [], []
    for piece in pieces:
        filt, send = call(
            filter_kernel,
            (shape(each, thick, ny, nx), shape(rows, nx)),
            [(3 * thick + 4, ny, nx)] * 2 + [(thick, ny, nx), (3 * thick + 4, ny, nx)],
            scalars=1,
        )(odd, *piece, pnear, potential, pfar)
        swapped = lax.all_to_all(send.reshape(groups, -1, 2, nx), ("z", "y", "x"), 0, 0)
        filtered.append(filt)
        received.append(swapped.reshape(rows, nx))

    size = groups * count
    parts = call(
        lambda *refs: gram_kernel(planes, each, *refs),
        shape(across * 4 * planes, 128),
        [(size, nx)] * 6,
    )(*received)

    plane = lax.all_to_all(parts.reshape(across, 4 * planes, 128), ("y", "x", "slab"), 0, 0)
    sums = call(spread_kernel, shape(planes * slabs, 4, 128))(plane)
    whole = lax.all_to_all(sums, ("z", "slab"), 0, 0)
    volume = 1.0 / (slabs * thick * ny * nx)
    correlation, projected = call(
        lambda *refs: finish_kernel(volume, *refs), (shape(slabs, 2 * 128), shape(slabs, 2 * 128))
    )(whole.reshape(planes, slabs * 4, 128))
    return jnp.concatenate(filtered, axis=0), correlation, projected


def solution(mesh):
    bands, slabs = mesh.devices.shape
    fine = Mesh(mesh.devices.reshape(bands // 8, 4, 2, slabs), ("z", "y", "x", "slab"))
    along = ("z", "y", "x")
    in_specs = (P(along, "slab", None, None), P("slab", None, None))
    out_specs = (P(along, "slab", None, None), P(along, None), P(along, None))
    return jax.shard_map(work, mesh=fine, in_specs=in_specs, out_specs=out_specs, check_vma=False)
```

profile of v0, /device:TPU:1, one launch (start us, length us, event | category | flops | bytes accessed | tf_op | source)
XLA Modules:
  0.0 97.3 jit_solution(5010517385168654015)
XLA Ops:
  0.6 0.0 copy-start
  0.6 4.2 %collective-permute-start.1 = (f32[4,8,24,128]{3,2,1,0:T(8,128)}, f32[4,8,24,128]{3,2,1,0:T(8,128)S(1)}, u32[]{:S(2)}, u32[]{:S(2)}) collective-permute-start(f32[4,8,24,128]{3,2,1,0:T(8,128)} %mid_ref.1), channel_id=1, source_target_pairs={{0,3},{3,0},{1,2},{2,1},{4,7},{7,4},{5,6},{6,5},{8,11},{11,8},{9,1... | collective-permute-start | bytes 1179656 | tf_op jit(solution)/shard_map/ppermute | solution.py:184
  4.8 0.0 collective-permute-start
  4.9 9.2 %collective-permute-done.1.far_ref = f32[4,8,24,128]{3,2,1,0:T(8,128)S(1)} collective-permute-done((f32[4,8,24,128]{3,2,1,0:T(8,128)}, f32[4,8,24,128]{3,2,1,0:T(8,128)S(1)}, u32[]{:S(2)}, u32[]{:S(2)}) %collective-permute-start.1) | collective-permute-done | bytes 393248 | tf_op jit(solution)/shard_map/ppermute | solution.py:184
  14.1 0.0 copy-start.1
  14.1 1.4 %collective-permute-start.2 = (f32[4,4,24,128]{3,2,1,0:T(8,128)S(1)}, f32[4,4,24,128]{3,2,1,0:T(8,128)S(1)}, u32[]{:S(2)}, u32[]{:S(2)}) collective-permute-start(f32[4,4,24,128]{3,2,1,0:T(8,128)S(1)} %pad_maximum_fusion), channel_id=1, source_target_pairs={{0,1},{1,0},{2,3},{3,2},{4,5},{5,4},{6,7},{7,6},{8,9},{9,8},{10,11... | collective-permute-start | bytes 589832 | tf_op jit(solution)/shard_map/ppermute | solution.py:187
  15.6 0.0 copy-done.1
  15.6 0.8 collective-permute-start.3
  16.3 2.7 %collective-permute-start.4 = (f32[8,24,128]{2,1,0:T(8,128)S(1)}, f32[8,24,128]{2,1,0:T(8,128)S(1)}, u32[]{:S(2)}, u32[]{:S(2)}) collective-permute-start(f32[8,24,128]{2,1,0:T(8,128)S(1)} %copy-done.1), channel_id=1, source_target_pairs={{0,3},{3,0},{1,2},{2,1},{4,7},{7,4},{5,6},{6,5},{8,11},{11,8},{9,1... | collective-permute-start | bytes 294920 | tf_op jit(solution)/shard_map/ppermute | solution.py:189
  19.0 0.0 collective-permute-done.3.pnear_ref
  19.0 3.3 %collective-permute-done.4.pfar_ref = f32[8,24,128]{2,1,0:T(8,128)S(1)} collective-permute-done((f32[8,24,128]{2,1,0:T(8,128)S(1)}, f32[8,24,128]{2,1,0:T(8,128)S(1)}, u32[]{:S(2)}, u32[]{:S(2)}) %collective-permute-start.4) | collective-permute-done | bytes 98336 | tf_op jit(solution)/shard_map/ppermute | solution.py:189
  22.3 0.0 collective-permute-done.near_ref
  22.3 0.0 collective-permute-done.2.ends_ref
  22.3 0.0 copy-done
  22.3 5.3 %shard_map.49 = (f32[4,8,24,128]{3,2,1,0:T(8,128)}, f32[1536,128]{1,0:T(8,128)S(1)}) custom-call(s32[1]{0:T(128)} %bitcast.odd_ref, f32[4,8,24,128]{3,2,1,0:T(8,128)S(1)} %collective-permute-done.near_ref, f32[4,8,24,128]{3,2,1,0:T(8,128)S(1)} %copy-done, f32[4,8,24,128]{3,2,1,0:T(8,128)S(1)} %collective-permute-done.1.far_ref, ...), custom_call_target="tpu_custom_call" | custom-call | tf_op jit(solution)/shard_map/pallas_call | solution.py:154
  27.5 34.0 %all_to_all.15 = f32[64,12,2,128]{3,2,1,0:T(2,128)S(1)} all-to-all(f32[64,12,2,128]{3,2,1,0:T(2,128)S(1)} %bitcast.7), channel_id=1, replica_groups=mesh['z'=8,'y'=4,'x'=2,'slab'=4] {'z','y','x'}, dimensions={0} | all-to-all | bytes 1572864 | tf_op jit(solution)/shard_map/all_to_all | solution.py:200
  61.5 1.3 %shard_map.50 = f32[1024,128]{1,0:T(8,128)S(1)} custom-call(f32[1536,128]{1,0:T(8,128)S(1)} %bitcast.5), custom_call_target="tpu_custom_call" | custom-call | tf_op jit(solution)/shard_map/pallas_call | solution.py:154
  62.8 19.8 %all_to_all.16.recv_ref = f32[32,32,128]{2,1,0:T(8,128)S(1)} all-to-all(f32[32,32,128]{2,1,0:T(8,128)S(1)} %bitcast.6), channel_id=1, replica_groups=mesh['z'=8,'y'=4,'x'=2,'slab'=4] {'y','x','slab'}, dimensions={0} | all-to-all | bytes 1048576 | tf_op jit(solution)/shard_map/all_to_all | solution.py:211
  82.6 14.1 %all_to_all.17 = f32[32,4,128]{2,1,0:T(4,128)S(1)} all-to-all(f32[32,4,128]{2,1,0:T(4,128)S(1)} %shard_map.51), channel_id=1, replica_groups=mesh['z'=8,'y'=4,'x'=2,'slab'=4] {'z','slab'}, dimensions={0} | all-to-all | bytes 131072 | tf_op jit(solution)/shard_map/all_to_all | solution.py:213
  96.7 0.6 shard_map.52
  (3 shorter events, 0.1 us)
Async XLA Ops:
  0.6 21.6 %copy-start = (f32[4,8,24,128]{3,2,1,0:T(8,128)S(1)}, f32[4,8,24,128]{3,2,1,0:T(8,128)}, u32[]{:S(2)}) copy-start(f32[4,8,24,128]{3,2,1,0:T(8,128)} %mid_ref.1) | copy-start | bytes 1179652
  0.6 13.4 %collective-permute-start.1 = (f32[4,8,24,128]{3,2,1,0:T(8,128)}, f32[4,8,24,128]{3,2,1,0:T(8,128)S(1)}, u32[]{:S(2)}, u32[]{:S(2)}) collective-permute-start(f32[4,8,24,128]{3,2,1,0:T(8,128)} %mid_ref.1), channel_id=1, source_target_pairs={{0,3},{3,0},{1,2},{2,1},{4,7},{7,4},{5,6},{6,5},{8,11},{11,8},{9,1... | collective-permute-start | bytes 1179656 | tf_op jit(solution)/shard_map/ppermute | solution.py:184
  4.8 17.4 %collective-permute-start = (f32[4,8,24,128]{3,2,1,0:T(8,128)}, f32[4,8,24,128]{3,2,1,0:T(8,128)S(1)}, u32[]{:S(2)}, u32[]{:S(2)}) collective-permute-start(f32[4,8,24,128]{3,2,1,0:T(8,128)} %mid_ref.1), channel_id=1, source_target_pairs={{0,1},{1,0},{2,3},{3,2},{4,5},{5,4},{6,7},{7,6},{8,9},{9,8},{10,11... | collective-permute-start | bytes 1179656 | tf_op jit(solution)/shard_map/ppermute | solution.py:185
  14.1 1.5 %copy-start.1 = (f32[8,24,128]{2,1,0:T(8,128)S(1)}, f32[8,24,128]{2,1,0:T(8,128)}, u32[]{:S(2)}) copy-start(f32[8,24,128]{2,1,0:T(8,128)} %pmid_ref.1) | copy-start | bytes 294916
  14.1 8.1 %collective-permute-start.2 = (f32[4,4,24,128]{3,2,1,0:T(8,128)S(1)}, f32[4,4,24,128]{3,2,1,0:T(8,128)S(1)}, u32[]{:S(2)}, u32[]{:S(2)}) collective-permute-start(f32[4,4,24,128]{3,2,1,0:T(8,128)S(1)} %pad_maximum_fusion), channel_id=1, source_target_pairs={{0,1},{1,0},{2,3},{3,2},{4,5},{5,4},{6,7},{7,6},{8,9},{9,8},{10,11... | collective-permute-start | bytes 589832 | tf_op jit(solution)/shard_map/ppermute | solution.py:187
  15.6 3.4 %collective-permute-start.3 = (f32[8,24,128]{2,1,0:T(8,128)S(1)}, f32[8,24,128]{2,1,0:T(8,128)S(1)}, u32[]{:S(2)}, u32[]{:S(2)}) collective-permute-start(f32[8,24,128]{2,1,0:T(8,128)S(1)} %copy-done.1), channel_id=1, source_target_pairs={{0,1},{1,0},{2,3},{3,2},{4,5},{5,4},{6,7},{7,6},{8,9},{9,8},{10,11... | collective-permute-start | bytes 294920 | tf_op jit(solution)/shard_map/ppermute | solution.py:190
  16.3 5.9 %collective-permute-start.4 = (f32[8,24,128]{2,1,0:T(8,128)S(1)}, f32[8,24,128]{2,1,0:T(8,128)S(1)}, u32[]{:S(2)}, u32[]{:S(2)}) collective-permute-start(f32[8,24,128]{2,1,0:T(8,128)S(1)} %copy-done.1), channel_id=1, source_target_pairs={{0,3},{3,0},{1,2},{2,1},{4,7},{7,4},{5,6},{6,5},{8,11},{11,8},{9,1... | collective-permute-start | bytes 294920 | tf_op jit(solution)/shard_map/ppermute | solution.py:189
where the time goes:
time: 97.5 us; the launch traced here: 97.3 us
  blocking collectives  67.8 us (70%)
  waiting for transfers between devices  12.5 us (13%)
  starting transfers between devices  9.06 us (9%)
  Pallas kernels  7.22 us (7%)
    all_to_all x1, blocking collectives, work(): lax.all_to_all(send.reshape(groups, -1, 2, nx), ('z', 'y', 'x'), 0, 0)  34 us
    all_to_all x1, blocking collectives, work(): lax.all_to_all(parts.reshape(across, 4 * planes, 128), ('y', 'x', 'slab')...  19.8 us
    all_to_all x1, blocking collectives, work(): whole = lax.all_to_all(sums, ('z', 'slab'), 0, 0)  14.1 us
    ppermute x1, waiting for transfers between devices, work(): other = lax.ppermute(mid, 'slab', far)  9.23 us
    pallas_call x4, Pallas kernels, run(): pl.pallas_call(kernel, out_shape=outs, in_specs=[pl.BlockSpec(memory_spac...  7.22 us
    ppermute x1, starting transfers between devices, work(): other = lax.ppermute(mid, 'slab', far)  4.21 us
    ppermute x1, waiting for transfers between devices, work(): pfar = lax.ppermute(potential, 'slab', far)  3.25 us
    ppermute x1, starting transfers between devices, work(): pfar = lax.ppermute(potential, 'slab', far)  2.65 us
  transfers between devices with their start and end apart: 5, of which 2 were waited for; matrix products, arithmetic and copies ran while one was open for 0% of the time, Pallas kernels for 0%

commit v1 on v0

--- a/solution.py
+++ b/solution.py
@@ -97,12 +97,11 @@
     lax.fori_loop(0, bands, one_band, 0)
 
 
-def gram_kernel(planes, per_chunk, *refs):
+def gram_kernel(per_chunk, *refs):
     recv_refs, out_ref, held = refs[:-7], refs[-7], refs[-6:]
     size = held[0].shape[0]
     bands = per_chunk * len(recv_refs)
     groups = size // bands
-    across = size // planes
     for f in range(2):
         for k in range(3):
             for band in range(bands):
@@ -120,27 +119,23 @@
             precision=lax.Precision.HIGHEST,
             preferred_element_type=jnp.float32,
         )
-        for z in range(planes):
-            for c in range(2):
-                part = block[z * across : (z + 1) * across, c * 128 : (c + 1) * 128]
-                out_ref[pl.ds((z * 2 + f) * 2 + c, across, stride=4 * planes), :] = part
-
-
-def spread_kernel(recv_ref, out_ref):
-    total = jnp.sum(recv_ref[...], axis=0)
-    planes = total.shape[0] // 4
-    for z in range(planes):
-        for s in range(4):
-            out_ref[z * 4 + s] = total[z * 4 : (z + 1) * 4]
-
-
-def finish_kernel(volume, recv_ref, corr_ref, proj_ref):
-    total = jnp.sum(recv_ref[...], axis=0) * volume
-    for s in range(4):
+        for c in range(2):
+            out_ref[pl.ds(f * 2 + c, size, stride=4), :] = block[:, c * 128 : (c + 1) * 128]
+
+
+def collect_kernel(recv_ref, out_ref):
+    out_ref[...] = jnp.sum(recv_ref[...], axis=0)
+
+
+def finish_kernel(volume, own_ref, next_ref, over_ref, last_ref, corr_ref, proj_ref):
+    total = (own_ref[...] + over_ref[...]) + (next_ref[...] + last_ref[...])
+    total = total * volume
+    for band in range(corr_ref.shape[0]):
         for c in range(2):
             lanes = slice(c * 128, (c + 1) * 128)
-            corr_ref[s : s + 1, lanes] = total[s * 4 + c : s * 4 + c + 1]
-            proj_ref[s : s + 1, lanes] = total[s * 4 + 2 + c : s * 4 + 3 + c]
+            row = band * 4 + c
+            corr_ref[band : band + 1, lanes] = total[row : row + 1]
+            proj_ref[band : band + 1, lanes] = total[row + 2 : row + 3]
 
 
 def shape(*dims):
@@ -168,9 +163,7 @@
 
 def work(bands, potential):
     slabs = lax.axis_size("slab")
-    planes = lax.axis_size("z")
-    across = lax.axis_size("y") * lax.axis_size("x") * slabs
-    groups = planes * across // slabs
+    groups = lax.axis_size("z") * lax.axis_size("y") * lax.axis_size("x")
     count, thick, ny, nx = bands.shape
     near = [(0, 1), (1, 0), (2, 3), (3, 2)]
     far = [(0, 3), (3, 0), (1, 2), (2, 1)]
@@ -203,18 +196,16 @@
 
     size = groups * count
     parts = call(
-        lambda *refs: gram_kernel(planes, each, *refs),
-        shape(across * 4 * planes, 128),
-        [(size, nx)] * 6,
+        lambda *refs: gram_kernel(each, *refs), shape(size * 4, 128), [(size, nx)] * 6
     )(*received)
 
-    plane = lax.all_to_all(parts.reshape(across, 4 * planes, 128), ("y", "x", "slab"), 0, 0)
-    sums = call(spread_kernel, shape(planes * slabs, 4, 128))(plane)
-    whole = lax.all_to_all(sums, ("z", "slab"), 0, 0)
+    swapped = lax.all_to_all(parts.reshape(groups, count * 4, 128), ("z", "y", "x"), 0, 0)
+    own = call(collect_kernel, shape(count * 4, 128))(swapped)
+    others = [lax.ppermute(own, "slab", [(i, (i + k) % slabs) for i in range(slabs)]) for k in (1, 2, 3)]
     volume = 1.0 / (slabs * thick * ny * nx)
     correlation, projected = call(
-        lambda *refs: finish_kernel(volume, *refs), (shape(slabs, 2 * 128), shape(slabs, 2 * 128))
-    )(whole.reshape(planes, slabs * 4, 128))
+        lambda *refs: finish_kernel(volume, *refs), (shape(count, 2 * 128), shape(count, 2 * 128))
+    )(own, *others)
     return jnp.concatenate(filtered, axis=0), correlation, projected
 
 

time: 97.5 us -> 94.7 us (0.971); the launches traced: 97.3 us -> 93.3 us
  blocking collectives: 67.8 us -> 55.9 us
  starting transfers between devices: 9.06 us -> 16.3 us
    all_to_all x2 -> x1, blocking collectives: 33.9 us -> 21.9 us  [work(): lax.all_to_all(parts.reshape(groups, count * 4, 128), ('z', 'y', 'x'), 0, 0)]
    ppermute x0 -> x3, starting transfers between devices: none -> 7.28 us  [work(): lax.ppermute(own, 'slab', [(i, (i + k) % slabs) for i in range(slabs)])]
  transfers between devices with their start and end apart: 5 -> 8, of which waited for: 2 -> 4; matrix products, arithmetic and copies ran while one was open for 0% -> 0% of each run, Pallas kernels for 0% -> 0%
where the time goes in v1:
time: 94.7 us; the launch traced here: 93.3 us
  blocking collectives  55.9 us (59%)
  starting transfers between devices  16.3 us (17%)
  waiting for transfers between devices  13.3 us (14%)
  Pallas kernels  7 us (7%)
    all_to_all x1, blocking collectives, work(): lax.all_to_all(send.reshape(groups, -1, 2, nx), ('z', 'y', 'x'), 0, 0)  34 us
    all_to_all x1, blocking collectives, work(): lax.all_to_all(parts.reshape(groups, count * 4, 128), ('z', 'y', 'x'), 0, 0)  21.9 us
    ppermute x1, waiting for transfers between devices, work(): other = lax.ppermute(mid, 'slab', far)  9.23 us
    ppermute x3, starting transfers between devices, work(): lax.ppermute(own, 'slab', [(i, (i + k) % slabs) for i in range(slabs)])  7.28 us
    pallas_call x4, Pallas kernels, run(): pl.pallas_call(kernel, out_shape=outs, in_specs=[pl.BlockSpec(memory_spac...  7 us
    ppermute x1, starting transfers between devices, work(): other = lax.ppermute(mid, 'slab', far)  4.21 us
    ppermute x1, waiting for transfers between devices, work(): pfar = lax.ppermute(potential, 'slab', far)  3.25 us
    ppermute x1, starting transfers between devices, work(): pfar = lax.ppermute(potential, 'slab', far)  2.65 us
  transfers between devices with their start and end apart: 8, of which 4 were waited for; matrix products, arithmetic and copies ran while one was open for 0% of the time, Pallas kernels for 0%

profile of v1, /device:TPU:1, one launch (start us, length us, event | category | flops | bytes accessed | tf_op | source)
XLA Modules:
  0.0 93.3 jit_solution(511948753752741919)
XLA Ops:
  0.6 0.0 copy-start
  0.6 4.2 %collective-permute-start.1 = (f32[4,8,24,128]{3,2,1,0:T(8,128)}, f32[4,8,24,128]{3,2,1,0:T(8,128)S(1)}, u32[]{:S(2)}, u32[]{:S(2)}) collective-permute-start(f32[4,8,24,128]{3,2,1,0:T(8,128)} %mid_ref.1), channel_id=1, source_target_pairs={{0,3},{3,0},{1,2},{2,1},{4,7},{7,4},{5,6},{6,5},{8,11},{11,8},{9,1... | collective-permute-start | bytes 1179656 | tf_op jit(solution)/shard_map/ppermute | solution.py:177
  4.8 0.0 collective-permute-start
  4.9 9.2 %collective-permute-done.1.far_ref = f32[4,8,24,128]{3,2,1,0:T(8,128)S(1)} collective-permute-done((f32[4,8,24,128]{3,2,1,0:T(8,128)}, f32[4,8,24,128]{3,2,1,0:T(8,128)S(1)}, u32[]{:S(2)}, u32[]{:S(2)}) %collective-permute-start.1) | collective-permute-done | bytes 393248 | tf_op jit(solution)/shard_map/ppermute | solution.py:177
  14.1 0.0 copy-start.1
  14.1 1.4 %collective-permute-start.2 = (f32[4,4,24,128]{3,2,1,0:T(8,128)S(1)}, f32[4,4,24,128]{3,2,1,0:T(8,128)S(1)}, u32[]{:S(2)}, u32[]{:S(2)}) collective-permute-start(f32[4,4,24,128]{3,2,1,0:T(8,128)S(1)} %pad_maximum_fusion), channel_id=1, source_target_pairs={{0,1},{1,0},{2,3},{3,2},{4,5},{5,4},{6,7},{7,6},{8,9},{9,8},{10,11... | collective-permute-start | bytes 589832 | tf_op jit(solution)/shard_map/ppermute | solution.py:180
  15.6 0.0 copy-done.1
  15.6 0.8 collective-permute-start.3
  16.3 2.7 %collective-permute-start.4 = (f32[8,24,128]{2,1,0:T(8,128)S(1)}, f32[8,24,128]{2,1,0:T(8,128)S(1)}, u32[]{:S(2)}, u32[]{:S(2)}) collective-permute-start(f32[8,24,128]{2,1,0:T(8,128)S(1)} %copy-done.1), channel_id=1, source_target_pairs={{0,3},{3,0},{1,2},{2,1},{4,7},{7,4},{5,6},{6,5},{8,11},{11,8},{9,1... | collective-permute-start | bytes 294920 | tf_op jit(solution)/shard_map/ppermute | solution.py:182
  19.0 0.0 collective-permute-done.3.pnear_ref
  19.0 3.3 %collective-permute-done.4.pfar_ref = f32[8,24,128]{2,1,0:T(8,128)S(1)} collective-permute-done((f32[8,24,128]{2,1,0:T(8,128)S(1)}, f32[8,24,128]{2,1,0:T(8,128)S(1)}, u32[]{:S(2)}, u32[]{:S(2)}) %collective-permute-start.4) | collective-permute-done | bytes 98336 | tf_op jit(solution)/shard_map/ppermute | solution.py:182
  22.3 0.0 collective-permute-done.near_ref
  22.3 0.0 collective-permute-done.2.ends_ref
  22.3 0.0 copy-done
  22.3 5.3 %shard_map.49 = (f32[4,8,24,128]{3,2,1,0:T(8,128)}, f32[1536,128]{1,0:T(8,128)S(1)}) custom-call(s32[1]{0:T(128)} %bitcast.odd_ref, f32[4,8,24,128]{3,2,1,0:T(8,128)S(1)} %collective-permute-done.near_ref, f32[4,8,24,128]{3,2,1,0:T(8,128)S(1)} %copy-done, f32[4,8,24,128]{3,2,1,0:T(8,128)S(1)} %collective-permute-done.1.far_ref, ...), custom_call_target="tpu_custom_call" | custom-call | tf_op jit(solution)/shard_map/pallas_call | solution.py:149
  27.5 34.0 %all_to_all.10 = f32[64,12,2,128]{3,2,1,0:T(2,128)S(1)} all-to-all(f32[64,12,2,128]{3,2,1,0:T(2,128)S(1)} %bitcast.6), channel_id=1, replica_groups=mesh['z'=8,'y'=4,'x'=2,'slab'=4] {'z','y','x'}, dimensions={0} | all-to-all | bytes 1572864 | tf_op jit(solution)/shard_map/all_to_all | solution.py:193
  61.5 1.1 %shard_map.50 = f32[1024,128]{1,0:T(8,128)S(1)} custom-call(f32[1536,128]{1,0:T(8,128)S(1)} %bitcast.4), custom_call_target="tpu_custom_call" | custom-call | tf_op jit(solution)/shard_map/pallas_call | solution.py:149
  62.6 21.9 %all_to_all.11.recv_ref = f32[64,16,128]{2,1,0:T(8,128)S(1)} all-to-all(f32[64,16,128]{2,1,0:T(8,128)S(1)} %bitcast.5), channel_id=1, replica_groups=mesh['z'=8,'y'=4,'x'=2,'slab'=4] {'z','y','x'}, dimensions={0} | all-to-all | bytes 1048576 | tf_op jit(solution)/shard_map/all_to_all | solution.py:202
  84.5 0.1 shard_map.51.refs_0_
  84.6 4.0 %collective-permute-start.7 = (f32[16,128]{1,0:T(8,128)S(1)}, f32[16,128]{1,0:T(8,128)S(1)}, u32[]{:S(2)}, u32[]{:S(2)}) collective-permute-start(f32[16,128]{1,0:T(8,128)S(1)} %shard_map.51.refs_0_), channel_id=1, source_target_pairs={{0,3},{1,0},{2,1},{3,2},{4,7},{5,4},{6,5},{7,6},{8,11},{9,8},{10,9... | collective-permute-start | bytes 24584 | tf_op jit(solution)/shard_map/ppermute | solution.py:204
  88.6 2.5 %collective-permute-start.6 = (f32[16,128]{1,0:T(8,128)S(1)}, f32[16,128]{1,0:T(8,128)S(1)}, u32[]{:S(2)}, u32[]{:S(2)}) collective-permute-start(f32[16,128]{1,0:T(8,128)S(1)} %shard_map.51.refs_0_), channel_id=1, source_target_pairs={{0,2},{1,3},{2,0},{3,1},{4,6},{5,7},{6,4},{7,5},{8,10},{9,11},{10,... | collective-permute-start | bytes 24584 | tf_op jit(solution)/shard_map/ppermute | solution.py:204
  91.1 0.8 collective-permute-start.5
  91.9 0.4 collective-permute-done.7.refs_3_
  92.3 0.3 collective-permute-done.6.refs_2_
  92.7 0.0 collective-permute-done.5.refs_1_
  92.7 0.6 shard_map.52
  (2 shorter events, 0.0 us)
Async XLA Ops:
  0.6 21.6 %copy-start = (f32[4,8,24,128]{3,2,1,0:T(8,128)S(1)}, f32[4,8,24,128]{3,2,1,0:T(8,128)}, u32[]{:S(2)}) copy-start(f32[4,8,24,128]{3,2,1,0:T(8,128)} %mid_ref.1) | copy-start | bytes 1179652
  0.6 13.4 %collective-permute-start.1 = (f32[4,8,24,128]{3,2,1,0:T(8,128)}, f32[4,8,24,128]{3,2,1,0:T(8,128)S(1)}, u32[]{:S(2)}, u32[]{:S(2)}) collective-permute-start(f32[4,8,24,128]{3,2,1,0:T(8,128)} %mid_ref.1), channel_id=1, source_target_pairs={{0,3},{3,0},{1,2},{2,1},{4,7},{7,4},{5,6},{6,5},{8,11},{11,8},{9,1... | collective-permute-start | bytes 1179656 | tf_op jit(solution)/shard_map/ppermute | solution.py:177
  4.8 17.4 %collective-permute-start = (f32[4,8,24,128]{3,2,1,0:T(8,128)}, f32[4,8,24,128]{3,2,1,0:T(8,128)S(1)}, u32[]{:S(2)}, u32[]{:S(2)}) collective-permute-start(f32[4,8,24,128]{3,2,1,0:T(8,128)} %mid_ref.1), channel_id=1, source_target_pairs={{0,1},{1,0},{2,3},{3,2},{4,5},{5,4},{6,7},{7,6},{8,9},{9,8},{10,11... | collective-permute-start | bytes 1179656 | tf_op jit(solution)/shard_map/ppermute | solution.py:178
  14.1 1.5 %copy-start.1 = (f32[8,24,128]{2,1,0:T(8,128)S(1)}, f32[8,24,128]{2,1,0:T(8,128)}, u32[]{:S(2)}) copy-start(f32[8,24,128]{2,1,0:T(8,128)} %pmid_ref.1) | copy-start | bytes 294916
  14.1 8.1 %collective-permute-start.2 = (f32[4,4,24,128]{3,2,1,0:T(8,128)S(1)}, f32[4,4,24,128]{3,2,1,0:T(8,128)S(1)}, u32[]{:S(2)}, u32[]{:S(2)}) collective-permute-start(f32[4,4,24,128]{3,2,1,0:T(8,128)S(1)} %pad_maximum_fusion), channel_id=1, source_target_pairs={{0,1},{1,0},{2,3},{3,2},{4,5},{5,4},{6,7},{7,6},{8,9},{9,8},{10,11... | collective-permute-start | bytes 589832 | tf_op jit(solution)/shard_map/ppermute | solution.py:180
  15.6 3.4 %collective-permute-start.3 = (f32[8,24,128]{2,1,0:T(8,128)S(1)}, f32[8,24,128]{2,1,0:T(8,128)S(1)}, u32[]{:S(2)}, u32[]{:S(2)}) collective-permute-start(f32[8,24,128]{2,1,0:T(8,128)S(1)} %copy-done.1), channel_id=1, source_target_pairs={{0,1},{1,0},{2,3},{3,2},{4,5},{5,4},{6,7},{7,6},{8,9},{9,8},{10,11... | collective-permute-start | bytes 294920 | tf_op jit(solution)/shard_map/ppermute | solution.py:183
  16.3 5.9 %collective-permute-start.4 = (f32[8,24,128]{2,1,0:T(8,128)S(1)}, f32[8,24,128]{2,1,0:T(8,128)S(1)}, u32[]{:S(2)}, u32[]{:S(2)}) collective-permute-start(f32[8,24,128]{2,1,0:T(8,128)S(1)} %copy-done.1), channel_id=1, source_target_pairs={{0,3},{3,0},{1,2},{2,1},{4,7},{7,4},{5,6},{6,5},{8,11},{11,8},{9,1... | collective-permute-start | bytes 294920 | tf_op jit(solution)/shard_map/ppermute | solution.py:182
  84.6 7.7 %collective-permute-start.7 = (f32[16,128]{1,0:T(8,128)S(1)}, f32[16,128]{1,0:T(8,128)S(1)}, u32[]{:S(2)}, u32[]{:S(2)}) collective-permute-start(f32[16,128]{1,0:T(8,128)S(1)} %shard_map.51.refs_0_), channel_id=1, source_target_pairs={{0,3},{1,0},{2,1},{3,2},{4,7},{5,4},{6,5},{7,6},{8,11},{9,8},{10,9... | collective-permute-start | bytes 24584 | tf_op jit(solution)/shard_map/ppermute | solution.py:204
  88.6 4.0 %collective-permute-start.6 = (f32[16,128]{1,0:T(8,128)S(1)}, f32[16,128]{1,0:T(8,128)S(1)}, u32[]{:S(2)}, u32[]{:S(2)}) collective-permute-start(f32[16,128]{1,0:T(8,128)S(1)} %shard_map.51.refs_0_), channel_id=1, source_target_pairs={{0,2},{1,3},{2,0},{3,1},{4,6},{5,7},{6,4},{7,5},{8,10},{9,11},{10,... | collective-permute-start | bytes 24584 | tf_op jit(solution)/shard_map/ppermute | solution.py:204
  91.1 1.6 %collective-permute-start.5 = (f32[16,128]{1,0:T(8,128)S(1)}, f32[16,128]{1,0:T(8,128)S(1)}, u32[]{:S(2)}, u32[]{:S(2)}) collective-permute-start(f32[16,128]{1,0:T(8,128)S(1)} %shard_map.51.refs_0_), channel_id=1, source_target_pairs={{0,1},{1,2},{2,3},{3,0},{4,5},{5,6},{6,7},{7,4},{8,9},{9,10},{10,1... | collective-permute-start | bytes 24584 | tf_op jit(solution)/shard_map/ppermute | solution.py:204

commit v2 on v1

v2 whole, which is shorter than its diff:
```python
import jax
import jax.numpy as jnp
import numpy as np
from jax import lax
from jax.experimental import pallas as pl
from jax.experimental.pallas import tpu as pltpu
from jax.sharding import Mesh, PartitionSpec as P


centre = 4.5
half = 3.5
scale = 2.0 / half

VMEM = pl.BlockSpec(memory_space=pltpu.VMEM)


BLOCK = 6


def stencil_matrices(ny, nx):
    depth = -(-(BLOCK + 4) * ny // 128) * 128
    yz = np.zeros((BLOCK, ny, depth), np.float32)
    for plane in range(BLOCK):
        for y in range(ny):
            for step, weight in ((1, -16.0), (2, 1.0)):
                for sign in (-step, step):
                    yz[plane, y, (plane + 2 + sign) * ny + y] += weight
                    yz[plane, y, (plane + 2) * ny + (y + sign) % ny] += weight
    x = np.zeros((nx, nx), np.float32)
    for column in range(nx):
        for step, weight in ((1, -16.0), (2, 1.0)):
            for sign in (-step, step):
                x[(column + sign) % nx, column] += weight
    return yz.reshape(BLOCK * ny, depth), np.concatenate([x, x])


def blocks(low, high):
    return [(z, min(BLOCK, high - z)) for z in range(low, high, BLOCK)]


def filter_kernel(odd_ref, yz_ref, x_ref, near_ref, mid_ref, outer_ref, inner_ref, ends_ref, *rest):
    pnear_ref, pmid_ref, pfar_ref, *rest = rest
    thick = mid_ref.shape[1]

    def own(ref):
        return lambda band, z: ref[band, z]

    def far(band, z):
        if 2 <= z < thick - 2:
            return inner_ref[band, (z - 2) // 2, z % 2]
        return outer_ref[band, z // (thick - 2), z % 2]

    def ends(band, z):
        return ends_ref[band, z // 2, z % 2]

    odd = odd_ref[0]

    @pl.when(odd == 0)
    def _():
        fields, pots = (far, own(mid_ref), own(near_ref)), (pfar_ref, pmid_ref, pnear_ref)
        filter_bands(mid_ref.shape, yz_ref, x_ref, fields, ends, pots, *rest)

    @pl.when(odd == 1)
    def _():
        fields, pots = (own(near_ref), own(mid_ref), far), (pnear_ref, pmid_ref, pfar_ref)
        filter_bands(mid_ref.shape, yz_ref, x_ref, fields, ends, pots, *rest)


def filter_bands(
    dims, yz_ref, x_ref, fields, ends, pots,
    filt_ref, send_ref,
    field_ref, split_ref, image_ref, weight_ref,
):
    bands, thick, ny, nx = dims
    edge = 2
    total = 3 * thick + 2 * edge
    own = thick + edge
    depth = yz_ref.shape[1]
    pad = split_ref.shape[2] - total * ny

    for part, ref in enumerate(pots):
        for z in range(thick):
            top = (edge + part * thick + z) * ny
            weight_ref[top : top + ny, :] = (ref[z] + (3.75 - centre)) * scale

    def split(into, top, height, value):
        for term, part in enumerate(terms(value)):
            split_ref[into, term, top : top + height, :] = part

    blank = jnp.zeros((pad + 2 * ny, 2 * nx), jnp.bfloat16)
    for into in range(2):
        for term in range(2):
            split_ref[into, term, (total - 2) * ny :, :] = blank

    def dot(left, right):
        return jnp.dot(left, right, preferred_element_type=jnp.float32)

    def step(level, z, planes):
        source = level % 2
        window = slice((z - 2) * ny, (z - 2) * ny + depth)
        here = slice(z * ny, (z + planes) * ny)
        weights = yz_ref[: planes * ny, :]
        near = dot(weights, split_ref[source, 0, window, :])
        near = near + dot(weights, split_ref[source, 1, window, :])
        lead, rest = split_ref[source, 0, here, :], split_ref[source, 1, here, :]
        along = [
            dot(jnp.concatenate([lead[:, lanes], rest[:, lanes]], axis=1), x_ref[...])
            for lanes in (slice(0, nx), slice(nx, 2 * nx))
        ]
        near = near + jnp.concatenate(along, axis=1)
        value = field_ref[level, here, :]
        weight = weight_ref[here, :]
        weight = jnp.concatenate([weight, weight], axis=1)
        return value, weight * value + (scale / 24.0) * near

    def pair(index, carry):
        first = index * 2
        for z in range(0, total, 2):
            if z < edge:
                get, at = ends, z + edge
            elif z >= total - edge:
                get, at = ends, z - (total - edge)
            else:
                get, at = fields[(z - edge) // thick], (z - edge) % thick
            value = jnp.concatenate(
                [
                    jnp.concatenate([get(first + band, at), get(first + band, at + 1)], axis=0)
                    for band in range(2)
                ],
                axis=1,
            )
            field_ref[0, z * ny : (z + 2) * ny, :] = value
            split(0, z * ny, 2 * ny, value)
        for level in range(4):
            for z, planes in blocks(2 * level + 2, total - 2 * level - 2):
                here = slice(z * ny, (z + planes) * ny)
                full = step(level, z, planes)[1]
                new = 0.5 * full if level == 0 else full - field_ref[level - 1, here, :]
                if level < 3:
                    field_ref[level + 1, here, :] = new
                else:
                    field_ref[4, here, :] = new
                    for plane in range(max(z, own), min(z + planes, own + thick)):
                        piece = new[(plane - z) * ny : (plane - z + 1) * ny]
                        for band in range(2):
                            filt_ref[first + band, plane - own] = piece[:, band * nx : (band + 1) * nx]
                split((level + 1) % 2, z * ny, planes * ny, new)
        for z, planes in blocks(own, own + thick):
            value, full = step(4, z, planes)
            new = (0.5 * half) * full + centre * value
            for plane in range(planes):
                piece = new[plane * ny : (plane + 1) * ny]
                for band in range(2):
                    image_ref[band, z + plane - own] = piece[:, band * nx : (band + 1) * nx]
        per = ny // 3
        for band in range(2):
            for z in range(thick):
                for f, at in enumerate((filt_ref.at[first + band, z], image_ref.at[band, z])):
                    for k in range(3):
                        line = ((z * per * bands + first + band) * 2 + f) * 3 + k
                        send_ref[pl.ds(line, per, stride=6 * bands), :] = at[pl.ds(k, per, stride=3), :]
        return carry

    lax.fori_loop(0, bands // 2, pair, 0)


def terms(value):
    lead = value.astype(jnp.bfloat16)
    return lead, (value - lead.astype(jnp.float32)).astype(jnp.bfloat16)


def gram_kernel(per_chunk, *refs):
    recv_refs, out_ref, held = refs[:-7], refs[-7], refs[-6:]
    size = held[0].shape[0]
    bands = per_chunk * len(recv_refs)
    groups = size // bands
    for f in range(2):
        for k in range(3):
            for band in range(bands):
                ref = recv_refs[band // per_chunk]
                first = ((band % per_chunk) * 2 + f) * 3 + k
                part = ref[pl.ds(first, groups, stride=6 * per_chunk), :]
                held[f * 3 + k][pl.ds(band, groups, stride=bands), :] = part
    filt, image = (
        terms(jnp.concatenate([ref[...] for ref in refs], axis=1)) for refs in (held[:3], held[3:])
    )
    right = jnp.concatenate([filt[0], filt[1], filt[0]], axis=1)
    for f, (lead, rest) in enumerate((filt, image)):
        block = lax.dot_general(
            jnp.concatenate([lead, lead, rest], axis=1),
            right,
            (((1,), (1,)), ((), ())),
            preferred_element_type=jnp.float32,
        )
        for c in range(2):
            out_ref[pl.ds(f * 2 + c, size, stride=4), :] = block[:, c * 128 : (c + 1) * 128]


def collect_kernel(recv_ref, out_ref):
    out_ref[...] = jnp.sum(recv_ref[...], axis=0)


def finish_kernel(volume, own_ref, next_ref, over_ref, last_ref, corr_ref, proj_ref):
    total = (own_ref[...] + over_ref[...]) + (next_ref[...] + last_ref[...])
    total = total * volume
    for band in range(corr_ref.shape[0]):
        for c in range(2):
            lanes = slice(c * 128, (c + 1) * 128)
            row = band * 4 + c
            corr_ref[band : band + 1, lanes] = total[row : row + 1]
            proj_ref[band : band + 1, lanes] = total[row + 2 : row + 3]


def shape(*dims):
    return jax.ShapeDtypeStruct(dims, jnp.float32)


def room(dims):
    kind = jnp.float32 if isinstance(dims[-1], int) else dims[-1]
    return pltpu.VMEM(tuple(d for d in dims if isinstance(d, int)), kind)


def call(kernel, outs, scratch=(), scalars=0):
    one = not isinstance(outs, tuple)

    def run(*args):
        return pl.pallas_call(
            kernel,
            out_shape=outs,
            in_specs=[pl.BlockSpec(memory_space=pltpu.SMEM)] * scalars + [VMEM] * (len(args) - scalars),
            out_specs=VMEM if one else (VMEM,) * len(outs),
            scratch_shapes=[room(dims) for dims in scratch],
            compiler_params=pltpu.CompilerParams(vmem_limit_bytes=16 * 2**20),
        )(*args)

    return run


def work(bands, potential):
    slabs = lax.axis_size("slab")
    groups = lax.axis_size("z") * lax.axis_size("y") * lax.axis_size("x")
    count, thick, ny, nx = bands.shape
    near = [(0, 1), (1, 0), (2, 3), (3, 2)]
    far = [(0, 3), (3, 0), (1, 2), (2, 1)]
    odd = jnp.reshape(lax.axis_index("slab") % 2, (1,)).astype(jnp.int32)
    rows = count * 2 * thick * ny

    pfar = lax.ppermute(potential, "slab", far)
    paired = bands.reshape(count, thick // 2, 2, ny, nx)
    outer = lax.ppermute(paired[:, :: thick // 2 - 1], "slab", far)
    inner = lax.ppermute(paired[:, 1:-1], "slab", far)
    beside = lax.ppermute(bands, "slab", near)
    pnear = lax.ppermute(potential, "slab", near)
    ends = lax.ppermute(outer, "slab", near)

    yz, x = (jnp.asarray(m, jnp.bfloat16) for m in stencil_matrices(ny, nx))
    deep = (3 * thick + 4) * ny + 64
    filtered, send = call(
        filter_kernel,
        (shape(count, thick, ny, nx), shape(rows, nx)),
        [
            (5, deep, 2 * nx),
            (2, 2, deep, 2 * nx, jnp.bfloat16),
            (2, thick, ny, nx),
            (deep, nx),
        ],
        scalars=1,
    )(odd, yz, x, beside, bands, outer, inner, ends, pnear, potential, pfar)
    swapped = lax.all_to_all(send.reshape(groups, -1, 2, nx), ("z", "y", "x"), 0, 0)
    received = swapped.reshape(rows, nx)

    size = groups * count
    parts = call(
        lambda *refs: gram_kernel(count, *refs), shape(size * 4, 128), [(size, nx)] * 6
    )(received)

    swapped = lax.all_to_all(parts.reshape(groups, count * 4, 128), ("z", "y", "x"), 0, 0)
    own = call(collect_kernel, shape(count * 4, 128))(swapped)
    others = [lax.ppermute(own, "slab", [(i, (i + k) % slabs) for i in range(slabs)]) for k in (1, 2, 3)]
    volume = 1.0 / (slabs * thick * ny * nx)
    correlation, projected = call(
        lambda *refs: finish_kernel(volume, *refs), (shape(count, 2 * 128), shape(count, 2 * 128))
    )(own, *others)
    return filtered, correlation, projected


def solution(mesh):
    bands, slabs = mesh.devices.shape
    fine = Mesh(mesh.devices.reshape(bands // 8, 4, 2, slabs), ("z", "y", "x", "slab"))
    along = ("z", "y", "x")
    in_specs = (P(along, "slab", None, None), P("slab", None, None))
    out_specs = (P(along, "slab", None, None), P(along, None), P(along, None))
    return jax.shard_map(work, mesh=fine, in_specs=in_specs, out_specs=out_specs, check_vma=False)
```

time: 94.7 us -> 89.1 us (0.941)
  waiting for transfers between devices: 13.3 us -> 7.61 us
  starting transfers between devices: 16.3 us -> 18.7 us
  Pallas kernels: 7 us -> 5.19 us
  blocking collectives: 55.9 us -> 54.4 us
  local copies, waits for them, and re-layouts: 0.02 us -> 1.13 us
    ppermute x3 -> x4, waiting for transfers between devices: 9.24 us -> 2.38 us  [the longest x1 2.37 us: work(): outer = lax.ppermute(paired[:, ::thick // 2 - 1], 'slab', far)]
    ppermute x3 -> x4, starting transfers between devices: 5.64 us -> 8.94 us  [the longest x1 4.21 us: work(): outer = lax.ppermute(paired[:, ::thick // 2 - 1], 'slab', far)]
    pallas_call x4, Pallas kernels: 7 us -> 5.19 us  [run(): pl.pallas_call(kernel, out_shape=outs, in_specs=[pl.BlockSpec(memory_spac...]
    all_to_all x1, blocking collectives: 34 us -> 32.5 us  [work(): lax.all_to_all(send.reshape(groups, -1, 2, nx), ('z', 'y', 'x'), 0, 0)]
    ppermute x1, waiting for transfers between devices: 3.25 us -> 4.44 us  [work(): pfar = lax.ppermute(potential, 'slab', far)]
    slice x1, local copies, waits for them, and re-layouts: 0.01 us -> 1.11 us  [work(): inner = lax.ppermute(paired[:, 1:-1], 'slab', far)]
  transfers between devices with their start and end apart: 8 -> 9, of which waited for: 4 -> 4; matrix products, arithmetic and copies ran while one was open for 0% -> 0% of each run, Pallas kernels for 0% -> 0%
where the time goes in v2:
time: 89.1 us; the launch traced here: 87.7 us
  blocking collectives  54.4 us (61%)
  starting transfers between devices  18.7 us (21%)
  waiting for transfers between devices  7.61 us (9%)
  Pallas kernels  5.19 us (6%)
  local copies, waits for them, and re-layouts  1.13 us (1%)
    all_to_all x1, blocking collectives, work(): lax.all_to_all(send.reshape(groups, -1, 2, nx), ('z', 'y', 'x'), 0, 0)  32.5 us
    all_to_all x1, blocking collectives, work(): lax.all_to_all(parts.reshape(groups, count * 4, 128), ('z', 'y', 'x'), 0, 0)  21.9 us
    ppermute x3, starting transfers between devices, work(): lax.ppermute(own, 'slab', [(i, (i + k) % slabs) for i in range(slabs)])  7.62 us
    pallas_call x4, Pallas kernels, run(): pl.pallas_call(kernel, out_shape=outs, in_specs=[pl.BlockSpec(memory_spac...  5.19 us
    ppermute x1, waiting for transfers between devices, work(): pfar = lax.ppermute(potential, 'slab', far)  4.44 us
    ppermute x1, starting transfers between devices, work(): outer = lax.ppermute(paired[:, ::thick // 2 - 1], 'slab', far)  4.21 us
    ppermute x1, starting transfers between devices, work(): ends = lax.ppermute(outer, 'slab', near)  2.41 us
    ppermute x1, waiting for transfers between devices, work(): outer = lax.ppermute(paired[:, ::thick // 2 - 1], 'slab', far)  2.37 us
  transfers between devices with their start and end apart: 9, of which 4 were waited for; matrix products, arithmetic and copies ran while one was open for 0% of the time, Pallas kernels for 0%

profile of v2, /device:TPU:1, one launch (start us, length us, event | category | flops | bytes accessed | tf_op | source)
XLA Modules:
  0.0 87.7 jit_solution(14374625946575961341)
XLA Ops:
  0.6 0.0 copy-start
  0.6 0.0 copy-start.1
  0.6 0.0 copy-start.2
  0.7 0.0 copy-start.3
  0.7 1.1 %fusion = (f32[4,2,2,24,128]{4,3,2,1,0:T(8,128)S(1)}, f32[4,2,2,24,128]{4,3,2,1,0:T(8,128)S(1)}) fusion(f32[4,4,2,24,128]{4,3,2,1,0:T(8,128)} %bitcast.7), kind=kLoop, calls=%fused_computation | loop fusion | bytes 786432 | tf_op jit(solution)/shard_map/slice | solution.py:251
  1.8 4.2 %collective-permute-start.1 = (f32[4,2,2,24,128]{4,3,2,1,0:T(8,128)S(1)}, f32[4,2,2,24,128]{4,3,2,1,0:T(8,128)S(1)}, u32[]{:S(2)}, u32[]{:S(2)}) collective-permute-start(f32[4,2,2,24,128]{4,3,2,1,0:T(8,128)S(1)} %get-tuple-element.12), channel_id=1, source_target_pairs={{0,3},{3,0},{1,2},{2,1},{4,7},{7,4},{5,6},{6,5},{8,11},{11,8},{9,1... | collective-permute-start | bytes 589832 | tf_op jit(solution)/shard_map/ppermute | solution.py:250
  6.0 0.0 copy-done
  6.0 0.0 collective-permute-start
  6.0 2.3 %collective-permute-start.2 = (f32[4,2,2,24,128]{4,3,2,1,0:T(8,128)S(1)}, f32[4,2,2,24,128]{4,3,2,1,0:T(8,128)S(1)}, u32[]{:S(2)}, u32[]{:S(2)}) collective-permute-start(f32[4,2,2,24,128]{4,3,2,1,0:T(8,128)S(1)} %get-tuple-element.11), channel_id=1, source_target_pairs={{0,3},{3,0},{1,2},{2,1},{4,7},{7,4},{5,6},{6,5},{8,11},{11,8},{9,1... | collective-permute-start | bytes 589832 | tf_op jit(solution)/shard_map/ppermute | solution.py:251
  8.3 2.4 %collective-permute-done.1.outer_ref = f32[4,2,2,24,128]{4,3,2,1,0:T(8,128)S(1)} collective-permute-done((f32[4,2,2,24,128]{4,3,2,1,0:T(8,128)S(1)}, f32[4,2,2,24,128]{4,3,2,1,0:T(8,128)S(1)}, u32[]{:S(2)}, u32[]{:S(2)}) %collective-permute-start.1) | collective-permute-done | bytes 196640 | tf_op jit(solution)/shard_map/ppermute | solution.py:250
  10.7 2.4 %collective-permute-start.3 = (f32[4,2,2,24,128]{4,3,2,1,0:T(8,128)S(1)}, f32[4,2,2,24,128]{4,3,2,1,0:T(8,128)S(1)}, u32[]{:S(2)}, u32[]{:S(2)}) collective-permute-start(f32[4,2,2,24,128]{4,3,2,1,0:T(8,128)S(1)} %collective-permute-done.1.outer_ref), channel_id=1, source_target_pairs={{0,1},{1,0},{2,3},{3,2},{4,5},{5,4},{6,7},{7,6},{8,9},{9,8},{10,11... | collective-permute-start | bytes 589832 | tf_op jit(solution)/shard_map/ppermute | solution.py:254
  13.1 0.0 copy-done.1
  13.1 0.0 collective-permute-start.4
  13.1 2.1 %collective-permute-start.5 = (f32[8,24,128]{2,1,0:T(8,128)S(1)}, f32[8,24,128]{2,1,0:T(8,128)S(1)}, u32[]{:S(2)}, u32[]{:S(2)}) collective-permute-start(f32[8,24,128]{2,1,0:T(8,128)S(1)} %copy-done.1), channel_id=1, source_target_pairs={{0,3},{3,0},{1,2},{2,1},{4,7},{7,4},{5,6},{6,5},{8,11},{11,8},{9,1... | collective-permute-start | bytes 294920 | tf_op jit(solution)/shard_map/ppermute | solution.py:248
  15.2 0.0 collective-permute-done.4.rest_0_
  15.2 4.4 %collective-permute-done.5.rest_2_ = f32[8,24,128]{2,1,0:T(8,128)S(1)} collective-permute-done((f32[8,24,128]{2,1,0:T(8,128)S(1)}, f32[8,24,128]{2,1,0:T(8,128)S(1)}, u32[]{:S(2)}, u32[]{:S(2)}) %collective-permute-start.5) | collective-permute-done | bytes 98336 | tf_op jit(solution)/shard_map/ppermute | solution.py:248
  19.6 0.0 collective-permute-done.2.inner_ref
  19.6 0.0 collective-permute-done.3.ends_ref
  19.6 0.0 collective-permute-done.near_ref
  19.7 0.0 copy-done.2
  19.7 3.9 %shard_map.67 = (f32[4,8,24,128]{3,2,1,0:T(8,128)}, f32[1536,128]{1,0:T(8,128)S(1)}) custom-call(s32[1]{0:T(128)} %bitcast.odd_ref, bf16[144,256]{1,0:T(8,128)(2,1)S(1)} %copy-done.2, bf16[256,128]{1,0:T(8,128)(2,1)S(1)} %copy-done.3, f32[4,8,24,128]{3,2,1,0:T(8,128)S(1)} %collective-permute-done.near_ref, f32[4,8,24,128]{3,2,1,0:T(8,128)S(1)} %copy-done, ...), custom_call_target="tpu_custom_call" | custom-call | tf_op jit(solution)/shard_map/pallas_call | solution.py:227
  23.6 32.5 %all_to_all.10 = f32[64,12,2,128]{3,2,1,0:T(2,128)S(1)} all-to-all(f32[64,12,2,128]{3,2,1,0:T(2,128)S(1)} %bitcast.8), channel_id=1, replica_groups=mesh['z'=8,'y'=4,'x'=2,'slab'=4] {'z','y','x'}, dimensions={0} | all-to-all | bytes 1572864 | tf_op jit(solution)/shard_map/all_to_all | solution.py:269
  56.1 0.6 shard_map.68
  56.7 21.9 %all_to_all.11.recv_ref = f32[64,16,128]{2,1,0:T(8,128)S(1)} all-to-all(f32[64,16,128]{2,1,0:T(8,128)S(1)} %bitcast.6), channel_id=1, replica_groups=mesh['z'=8,'y'=4,'x'=2,'slab'=4] {'z','y','x'}, dimensions={0} | all-to-all | bytes 1048576 | tf_op jit(solution)/shard_map/all_to_all | solution.py:277
  78.6 0.1 shard_map.69.refs_0_
  78.6 4.4 %collective-permute-start.8 = (f32[16,128]{1,0:T(8,128)S(1)}, f32[16,128]{1,0:T(8,128)S(1)}, u32[]{:S(2)}, u32[]{:S(2)}) collective-permute-start(f32[16,128]{1,0:T(8,128)S(1)} %shard_map.69.refs_0_), channel_id=1, source_target_pairs={{0,3},{1,0},{2,1},{3,2},{4,7},{5,4},{6,5},{7,6},{8,11},{9,8},{10,9... | collective-permute-start | bytes 24584 | tf_op jit(solution)/shard_map/ppermute | solution.py:279
  83.0 2.5 %collective-permute-start.7 = (f32[16,128]{1,0:T(8,128)S(1)}, f32[16,128]{1,0:T(8,128)S(1)}, u32[]{:S(2)}, u32[]{:S(2)}) collective-permute-start(f32[16,128]{1,0:T(8,128)S(1)} %shard_map.69.refs_0_), channel_id=1, source_target_pairs={{0,2},{1,3},{2,0},{3,1},{4,6},{5,7},{6,4},{7,5},{8,10},{9,11},{10,... | collective-permute-start | bytes 24584 | tf_op jit(solution)/shard_map/ppermute | solution.py:279
  85.5 0.8 collective-permute-start.6
  86.3 0.4 collective-permute-done.8.refs_3_
  86.7 0.3 collective-permute-done.7.refs_2_
  87.0 0.0 collective-permute-done.6.refs_1_
  87.1 0.6 shard_map.70
  (1 shorter events, 0.0 us)
Async XLA Ops:
  0.6 5.4 %copy-start = (f32[4,8,24,128]{3,2,1,0:T(8,128)S(1)}, f32[4,8,24,128]{3,2,1,0:T(8,128)}, u32[]{:S(2)}) copy-start(f32[4,8,24,128]{3,2,1,0:T(8,128)} %mid_ref.1) | copy-start | bytes 1179652
  0.6 12.5 %copy-start.1 = (f32[8,24,128]{2,1,0:T(8,128)S(1)}, f32[8,24,128]{2,1,0:T(8,128)}, u32[]{:S(2)}) copy-start(f32[8,24,128]{2,1,0:T(8,128)} %rest_1_.1) | copy-start | bytes 294916
  0.6 19.0 %copy-start.2 = (bf16[144,256]{1,0:T(8,128)(2,1)S(1)}, bf16[144,256]{1,0:T(8,128)(2,1)}, u32[]{:S(2)}) copy-start(bf16[144,256]{1,0:T(8,128)(2,1)} %constant.21.clone.yz_ref) | copy-start | bytes 221188
  0.7 19.0 %copy-start.3 = (bf16[256,128]{1,0:T(8,128)(2,1)S(1)}, bf16[256,128]{1,0:T(8,128)(2,1)}, u32[]{:S(2)}) copy-start(bf16[256,128]{1,0:T(8,128)(2,1)} %constant.22.clone.x_ref) | copy-start | bytes 196612
  1.8 8.9 %collective-permute-start.1 = (f32[4,2,2,24,128]{4,3,2,1,0:T(8,128)S(1)}, f32[4,2,2,24,128]{4,3,2,1,0:T(8,128)S(1)}, u32[]{:S(2)}, u32[]{:S(2)}) collective-permute-start(f32[4,2,2,24,128]{4,3,2,1,0:T(8,128)S(1)} %get-tuple-element.12), channel_id=1, source_target_pairs={{0,3},{3,0},{1,2},{2,1},{4,7},{7,4},{5,6},{6,5},{8,11},{11,8},{9,1... | collective-permute-start | bytes 589832 | tf_op jit(solution)/shard_map/ppermute | solution.py:250
  6.0 13.7 %collective-permute-start = (f32[4,8,24,128]{3,2,1,0:T(8,128)S(1)}, f32[4,8,24,128]{3,2,1,0:T(8,128)S(1)}, u32[]{:S(2)}, u32[]{:S(2)}) collective-permute-start(f32[4,8,24,128]{3,2,1,0:T(8,128)S(1)} %copy-done), channel_id=1, source_target_pairs={{0,1},{1,0},{2,3},{3,2},{4,5},{5,4},{6,7},{7,6},{8,9},{9,8},{10,11... | collective-permute-start | bytes 1179656 | tf_op jit(solution)/shard_map/ppermute | solution.py:252
  6.0 13.6 %collective-permute-start.2 = (f32[4,2,2,24,128]{4,3,2,1,0:T(8,128)S(1)}, f32[4,2,2,24,128]{4,3,2,1,0:T(8,128)S(1)}, u32[]{:S(2)}, u32[]{:S(2)}) collective-permute-start(f32[4,2,2,24,128]{4,3,2,1,0:T(8,128)S(1)} %get-tuple-element.11), channel_id=1, source_target_pairs={{0,3},{3,0},{1,2},{2,1},{4,7},{7,4},{5,6},{6,5},{8,11},{11,8},{9,1... | collective-permute-start | bytes 589832 | tf_op jit(solution)/shard_map/ppermute | solution.py:251
  10.7 8.9 %collective-permute-start.3 = (f32[4,2,2,24,128]{4,3,2,1,0:T(8,128)S(1)}, f32[4,2,2,24,128]{4,3,2,1,0:T(8,128)S(1)}, u32[]{:S(2)}, u32[]{:S(2)}) collective-permute-start(f32[4,2,2,24,128]{4,3,2,1,0:T(8,128)S(1)} %collective-permute-done.1.outer_ref), channel_id=1, source_target_pairs={{0,1},{1,0},{2,3},{3,2},{4,5},{5,4},{6,7},{7,6},{8,9},{9,8},{10,11... | collective-permute-start | bytes 589832 | tf_op jit(solution)/shard_map/ppermute | solution.py:254
  13.1 2.1 %collective-permute-start.4 = (f32[8,24,128]{2,1,0:T(8,128)S(1)}, f32[8,24,128]{2,1,0:T(8,128)S(1)}, u32[]{:S(2)}, u32[]{:S(2)}) collective-permute-start(f32[8,24,128]{2,1,0:T(8,128)S(1)} %copy-done.1), channel_id=1, source_target_pairs={{0,1},{1,0},{2,3},{3,2},{4,5},{5,4},{6,7},{7,6},{8,9},{9,8},{10,11... | collective-permute-start | bytes 294920 | tf_op jit(solution)/shard_map/ppermute | solution.py:253
  13.1 6.5 %collective-permute-start.5 = (f32[8,24,128]{2,1,0:T(8,128)S(1)}, f32[8,24,128]{2,1,0:T(8,128)S(1)}, u32[]{:S(2)}, u32[]{:S(2)}) collective-permute-start(f32[8,24,128]{2,1,0:T(8,128)S(1)} %copy-done.1), channel_id=1, source_target_pairs={{0,3},{3,0},{1,2},{2,1},{4,7},{7,4},{5,6},{6,5},{8,11},{11,8},{9,1... | collective-permute-start | bytes 294920 | tf_op jit(solution)/shard_map/ppermute | solution.py:248
  78.6 8.1 %collective-permute-start.8 = (f32[16,128]{1,0:T(8,128)S(1)}, f32[16,128]{1,0:T(8,128)S(1)}, u32[]{:S(2)}, u32[]{:S(2)}) collective-permute-start(f32[16,128]{1,0:T(8,128)S(1)} %shard_map.69.refs_0_), channel_id=1, source_target_pairs={{0,3},{1,0},{2,1},{3,2},{4,7},{5,4},{6,5},{7,6},{8,11},{9,8},{10,9... | collective-permute-start | bytes 24584 | tf_op jit(solution)/shard_map/ppermute | solution.py:279
  83.0 4.0 %collective-permute-start.7 = (f32[16,128]{1,0:T(8,128)S(1)}, f32[16,128]{1,0:T(8,128)S(1)}, u32[]{:S(2)}, u32[]{:S(2)}) collective-permute-start(f32[16,128]{1,0:T(8,128)S(1)} %shard_map.69.refs_0_), channel_id=1, source_target_pairs={{0,2},{1,3},{2,0},{3,1},{4,6},{5,7},{6,4},{7,5},{8,10},{9,11},{10,... | collective-permute-start | bytes 24584 | tf_op jit(solution)/shard_map/ppermute | solution.py:279
  85.5 1.6 %collective-permute-start.6 = (f32[16,128]{1,0:T(8,128)S(1)}, f32[16,128]{1,0:T(8,128)S(1)}, u32[]{:S(2)}, u32[]{:S(2)}) collective-permute-start(f32[16,128]{1,0:T(8,128)S(1)} %shard_map.69.refs_0_), channel_id=1, source_target_pairs={{0,1},{1,2},{2,3},{3,0},{4,5},{5,6},{6,7},{7,4},{8,9},{9,10},{10,1... | collective-permute-start | bytes 24584 | tf_op jit(solution)/shard_map/ppermute | solution.py:279

commit v3 on v2

--- a/solution.py
+++ b/solution.py
@@ -200,8 +200,8 @@
     out_ref[...] = jnp.sum(recv_ref[...], axis=0)
 
 
-def finish_kernel(volume, own_ref, next_ref, over_ref, last_ref, corr_ref, proj_ref):
-    total = (own_ref[...] + over_ref[...]) + (next_ref[...] + last_ref[...])
+def finish_kernel(volume, own_ref, near_ref, over_ref, far_ref, corr_ref, proj_ref):
+    total = (own_ref[...] + over_ref[...]) + (near_ref[...] + far_ref[...])
     total = total * volume
     for band in range(corr_ref.shape[0]):
         for c in range(2):
@@ -276,11 +276,14 @@
 
     swapped = lax.all_to_all(parts.reshape(groups, count * 4, 128), ("z", "y", "x"), 0, 0)
     own = call(collect_kernel, shape(count * 4, 128))(swapped)
-    others = [lax.ppermute(own, "slab", [(i, (i + k) % slabs) for i in range(slabs)]) for k in (1, 2, 3)]
+    over = [(i, (i + 2) % slabs) for i in range(slabs)]
+    distant = lax.ppermute(own, "slab", far)
+    opposite = lax.ppermute(own, "slab", over)
+    sibling = lax.ppermute(own, "slab", near)
     volume = 1.0 / (slabs * thick * ny * nx)
     correlation, projected = call(
         lambda *refs: finish_kernel(volume, *refs), (shape(count, 2 * 128), shape(count, 2 * 128))
-    )(own, *others)
+    )(own, sibling, opposite, distant)
     return filtered, correlation, projected
 
 

time: 89.1 us -> 90.2 us (1.012); the launches traced: 87.7 us -> 90 us
  waiting for transfers between devices: 7.61 us -> 10.3 us
    ppermute x3, waiting for transfers between devices: 0.79 us -> 3.49 us  [the longest x1 2.67 us: work(): opposite = lax.ppermute(own, 'slab', over)]
where the time goes in v3:
time: 90.2 us; the launch traced here: 90 us
  blocking collectives  54.4 us (60%)
  starting transfers between devices  18.3 us (20%)
  waiting for transfers between devices  10.3 us (11%)
  Pallas kernels  5.19 us (6%)
  local copies, waits for them, and re-layouts  1.13 us (1%)
    all_to_all x1, blocking collectives, work(): lax.all_to_all(send.reshape(groups, -1, 2, nx), ('z', 'y', 'x'), 0, 0)  32.5 us
    all_to_all x1, blocking collectives, work(): lax.all_to_all(parts.reshape(groups, count * 4, 128), ('z', 'y', 'x'), 0, 0)  21.9 us
    ppermute x1, starting transfers between devices, work(): distant = lax.ppermute(own, 'slab', far)  6.73 us
    pallas_call x4, Pallas kernels, run(): pl.pallas_call(kernel, out_shape=outs, in_specs=[pl.BlockSpec(memory_spac...  5.19 us
    ppermute x1, waiting for transfers between devices, work(): pfar = lax.ppermute(potential, 'slab', far)  4.44 us
    ppermute x1, starting transfers between devices, work(): outer = lax.ppermute(paired[:, ::thick // 2 - 1], 'slab', far)  4.21 us
    ppermute x1, waiting for transfers between devices, work(): opposite = lax.ppermute(own, 'slab', over)  2.67 us
    ppermute x1, starting transfers between devices, work(): ends = lax.ppermute(outer, 'slab', near)  2.41 us
  transfers between devices with their start and end apart: 9, of which 4 were waited for; matrix products, arithmetic and copies ran while one was open for 0% of the time, Pallas kernels for 0%

profile of v3, /device:TPU:1, one launch (start us, length us, event | category | flops | bytes accessed | tf_op | source)
XLA Modules:
  0.0 90.0 jit_solution(7802549605065565167)
XLA Ops:
  0.6 0.0 copy-start
  0.6 0.0 copy-start.1
  0.6 0.0 copy-start.2
  0.7 0.0 copy-start.3
  0.7 1.1 %fusion = (f32[4,2,2,24,128]{4,3,2,1,0:T(8,128)S(1)}, f32[4,2,2,24,128]{4,3,2,1,0:T(8,128)S(1)}) fusion(f32[4,4,2,24,128]{4,3,2,1,0:T(8,128)} %bitcast.7), kind=kLoop, calls=%fused_computation | loop fusion | bytes 786432 | tf_op jit(solution)/shard_map/slice | solution.py:251
  1.8 4.2 %collective-permute-start.1 = (f32[4,2,2,24,128]{4,3,2,1,0:T(8,128)S(1)}, f32[4,2,2,24,128]{4,3,2,1,0:T(8,128)S(1)}, u32[]{:S(2)}, u32[]{:S(2)}) collective-permute-start(f32[4,2,2,24,128]{4,3,2,1,0:T(8,128)S(1)} %get-tuple-element.12), channel_id=1, source_target_pairs={{0,3},{3,0},{1,2},{2,1},{4,7},{7,4},{5,6},{6,5},{8,11},{11,8},{9,1... | collective-permute-start | bytes 589832 | tf_op jit(solution)/shard_map/ppermute | solution.py:250
  6.0 0.0 copy-done
  6.0 0.0 collective-permute-start
  6.0 2.3 %collective-permute-start.2 = (f32[4,2,2,24,128]{4,3,2,1,0:T(8,128)S(1)}, f32[4,2,2,24,128]{4,3,2,1,0:T(8,128)S(1)}, u32[]{:S(2)}, u32[]{:S(2)}) collective-permute-start(f32[4,2,2,24,128]{4,3,2,1,0:T(8,128)S(1)} %get-tuple-element.11), channel_id=1, source_target_pairs={{0,3},{3,0},{1,2},{2,1},{4,7},{7,4},{5,6},{6,5},{8,11},{11,8},{9,1... | collective-permute-start | bytes 589832 | tf_op jit(solution)/shard_map/ppermute | solution.py:251
  8.3 2.4 %collective-permute-done.1.outer_ref = f32[4,2,2,24,128]{4,3,2,1,0:T(8,128)S(1)} collective-permute-done((f32[4,2,2,24,128]{4,3,2,1,0:T(8,128)S(1)}, f32[4,2,2,24,128]{4,3,2,1,0:T(8,128)S(1)}, u32[]{:S(2)}, u32[]{:S(2)}) %collective-permute-start.1) | collective-permute-done | bytes 196640 | tf_op jit(solution)/shard_map/ppermute | solution.py:250
  10.7 2.4 %collective-permute-start.3 = (f32[4,2,2,24,128]{4,3,2,1,0:T(8,128)S(1)}, f32[4,2,2,24,128]{4,3,2,1,0:T(8,128)S(1)}, u32[]{:S(2)}, u32[]{:S(2)}) collective-permute-start(f32[4,2,2,24,128]{4,3,2,1,0:T(8,128)S(1)} %collective-permute-done.1.outer_ref), channel_id=1, source_target_pairs={{0,1},{1,0},{2,3},{3,2},{4,5},{5,4},{6,7},{7,6},{8,9},{9,8},{10,11... | collective-permute-start | bytes 589832 | tf_op jit(solution)/shard_map/ppermute | solution.py:254
  13.1 0.0 copy-done.1
  13.1 0.0 collective-permute-start.4
  13.1 2.1 %collective-permute-start.5 = (f32[8,24,128]{2,1,0:T(8,128)S(1)}, f32[8,24,128]{2,1,0:T(8,128)S(1)}, u32[]{:S(2)}, u32[]{:S(2)}) collective-permute-start(f32[8,24,128]{2,1,0:T(8,128)S(1)} %copy-done.1), channel_id=1, source_target_pairs={{0,3},{3,0},{1,2},{2,1},{4,7},{7,4},{5,6},{6,5},{8,11},{11,8},{9,1... | collective-permute-start | bytes 294920 | tf_op jit(solution)/shard_map/ppermute | solution.py:248
  15.2 0.0 collective-permute-done.4.rest_0_
  15.2 4.4 %collective-permute-done.5.rest_2_ = f32[8,24,128]{2,1,0:T(8,128)S(1)} collective-permute-done((f32[8,24,128]{2,1,0:T(8,128)S(1)}, f32[8,24,128]{2,1,0:T(8,128)S(1)}, u32[]{:S(2)}, u32[]{:S(2)}) %collective-permute-start.5) | collective-permute-done | bytes 98336 | tf_op jit(solution)/shard_map/ppermute | solution.py:248
  19.6 0.0 collective-permute-done.2.inner_ref
  19.6 0.0 collective-permute-done.3.ends_ref
  19.6 0.0 collective-permute-done.near_ref
  19.7 0.0 copy-done.2
  19.7 3.9 %shard_map.67 = (f32[4,8,24,128]{3,2,1,0:T(8,128)}, f32[1536,128]{1,0:T(8,128)S(1)}) custom-call(s32[1]{0:T(128)} %bitcast.odd_ref, bf16[144,256]{1,0:T(8,128)(2,1)S(1)} %copy-done.2, bf16[256,128]{1,0:T(8,128)(2,1)S(1)} %copy-done.3, f32[4,8,24,128]{3,2,1,0:T(8,128)S(1)} %collective-permute-done.near_ref, f32[4,8,24,128]{3,2,1,0:T(8,128)S(1)} %copy-done, ...), custom_call_target="tpu_custom_call" | custom-call | tf_op jit(solution)/shard_map/pallas_call | solution.py:227
  23.6 32.5 %all_to_all.10 = f32[64,12,2,128]{3,2,1,0:T(2,128)S(1)} all-to-all(f32[64,12,2,128]{3,2,1,0:T(2,128)S(1)} %bitcast.8), channel_id=1, replica_groups=mesh['z'=8,'y'=4,'x'=2,'slab'=4] {'z','y','x'}, dimensions={0} | all-to-all | bytes 1572864 | tf_op jit(solution)/shard_map/all_to_all | solution.py:269
  56.1 0.6 shard_map.68
  56.7 21.9 %all_to_all.11.recv_ref = f32[64,16,128]{2,1,0:T(8,128)S(1)} all-to-all(f32[64,16,128]{2,1,0:T(8,128)S(1)} %bitcast.6), channel_id=1, replica_groups=mesh['z'=8,'y'=4,'x'=2,'slab'=4] {'z','y','x'}, dimensions={0} | all-to-all | bytes 1048576 | tf_op jit(solution)/shard_map/all_to_all | solution.py:277
  78.6 0.1 shard_map.69.refs_0_
  78.6 6.7 %collective-permute-start.8 = (f32[16,128]{1,0:T(8,128)S(1)}, f32[16,128]{1,0:T(8,128)S(1)}, u32[]{:S(2)}, u32[]{:S(2)}) collective-permute-start(f32[16,128]{1,0:T(8,128)S(1)} %shard_map.69.refs_0_), channel_id=1, source_target_pairs={{0,3},{3,0},{1,2},{2,1},{4,7},{7,4},{5,6},{6,5},{8,11},{11,8},{9,1... | collective-permute-start | bytes 24584 | tf_op jit(solution)/shard_map/ppermute | solution.py:280
  85.4 0.5 collective-permute-start.7
  85.9 0.0 collective-permute-start.6
  85.9 0.8 collective-permute-done.8.refs_3_
  86.7 2.7 %collective-permute-done.7.refs_2_ = f32[16,128]{1,0:T(8,128)S(1)} collective-permute-done((f32[16,128]{1,0:T(8,128)S(1)}, f32[16,128]{1,0:T(8,128)S(1)}, u32[]{:S(2)}, u32[]{:S(2)}) %collective-permute-start.7) | collective-permute-done | bytes 8224 | tf_op jit(solution)/shard_map/ppermute | solution.py:281
  89.4 0.0 collective-permute-done.6.refs_1_
  89.4 0.6 shard_map.70
  (1 shorter events, 0.0 us)
Async XLA Ops:
  0.6 5.4 %copy-start = (f32[4,8,24,128]{3,2,1,0:T(8,128)S(1)}, f32[4,8,24,128]{3,2,1,0:T(8,128)}, u32[]{:S(2)}) copy-start(f32[4,8,24,128]{3,2,1,0:T(8,128)} %mid_ref.1) | copy-start | bytes 1179652
  0.6 12.5 %copy-start.1 = (f32[8,24,128]{2,1,0:T(8,128)S(1)}, f32[8,24,128]{2,1,0:T(8,128)}, u32[]{:S(2)}) copy-start(f32[8,24,128]{2,1,0:T(8,128)} %rest_1_.1) | copy-start | bytes 294916
  0.6 19.0 %copy-start.2 = (bf16[144,256]{1,0:T(8,128)(2,1)S(1)}, bf16[144,256]{1,0:T(8,128)(2,1)}, u32[]{:S(2)}) copy-start(bf16[144,256]{1,0:T(8,128)(2,1)} %constant.21.clone.yz_ref) | copy-start | bytes 221188
  0.7 19.0 %copy-start.3 = (bf16[256,128]{1,0:T(8,128)(2,1)S(1)}, bf16[256,128]{1,0:T(8,128)(2,1)}, u32[]{:S(2)}) copy-start(bf16[256,128]{1,0:T(8,128)(2,1)} %constant.22.clone.x_ref) | copy-start | bytes 196612
  1.8 8.9 %collective-permute-start.1 = (f32[4,2,2,24,128]{4,3,2,1,0:T(8,128)S(1)}, f32[4,2,2,24,128]{4,3,2,1,0:T(8,128)S(1)}, u32[]{:S(2)}, u32[]{:S(2)}) collective-permute-start(f32[4,2,2,24,128]{4,3,2,1,0:T(8,128)S(1)} %get-tuple-element.12), channel_id=1, source_target_pairs={{0,3},{3,0},{1,2},{2,1},{4,7},{7,4},{5,6},{6,5},{8,11},{11,8},{9,1... | collective-permute-start | bytes 589832 | tf_op jit(solution)/shard_map/ppermute | solution.py:250
  6.0 13.7 %collective-permute-start = (f32[4,8,24,128]{3,2,1,0:T(8,128)S(1)}, f32[4,8,24,128]{3,2,1,0:T(8,128)S(1)}, u32[]{:S(2)}, u32[]{:S(2)}) collective-permute-start(f32[4,8,24,128]{3,2,1,0:T(8,128)S(1)} %copy-done), channel_id=1, source_target_pairs={{0,1},{1,0},{2,3},{3,2},{4,5},{5,4},{6,7},{7,6},{8,9},{9,8},{10,11... | collective-permute-start | bytes 1179656 | tf_op jit(solution)/shard_map/ppermute | solution.py:252
  6.0 13.6 %collective-permute-start.2 = (f32[4,2,2,24,128]{4,3,2,1,0:T(8,128)S(1)}, f32[4,2,2,24,128]{4,3,2,1,0:T(8,128)S(1)}, u32[]{:S(2)}, u32[]{:S(2)}) collective-permute-start(f32[4,2,2,24,128]{4,3,2,1,0:T(8,128)S(1)} %get-tuple-element.11), channel_id=1, source_target_pairs={{0,3},{3,0},{1,2},{2,1},{4,7},{7,4},{5,6},{6,5},{8,11},{11,8},{9,1... | collective-permute-start | bytes 589832 | tf_op jit(solution)/shard_map/ppermute | solution.py:251
  10.7 8.9 %collective-permute-start.3 = (f32[4,2,2,24,128]{4,3,2,1,0:T(8,128)S(1)}, f32[4,2,2,24,128]{4,3,2,1,0:T(8,128)S(1)}, u32[]{:S(2)}, u32[]{:S(2)}) collective-permute-start(f32[4,2,2,24,128]{4,3,2,1,0:T(8,128)S(1)} %collective-permute-done.1.outer_ref), channel_id=1, source_target_pairs={{0,1},{1,0},{2,3},{3,2},{4,5},{5,4},{6,7},{7,6},{8,9},{9,8},{10,11... | collective-permute-start | bytes 589832 | tf_op jit(solution)/shard_map/ppermute | solution.py:254
  13.1 2.1 %collective-permute-start.4 = (f32[8,24,128]{2,1,0:T(8,128)S(1)}, f32[8,24,128]{2,1,0:T(8,128)S(1)}, u32[]{:S(2)}, u32[]{:S(2)}) collective-permute-start(f32[8,24,128]{2,1,0:T(8,128)S(1)} %copy-done.1), channel_id=1, source_target_pairs={{0,1},{1,0},{2,3},{3,2},{4,5},{5,4},{6,7},{7,6},{8,9},{9,8},{10,11... | collective-permute-start | bytes 294920 | tf_op jit(solution)/shard_map/ppermute | solution.py:253
  13.1 6.5 %collective-permute-start.5 = (f32[8,24,128]{2,1,0:T(8,128)S(1)}, f32[8,24,128]{2,1,0:T(8,128)S(1)}, u32[]{:S(2)}, u32[]{:S(2)}) collective-permute-start(f32[8,24,128]{2,1,0:T(8,128)S(1)} %copy-done.1), channel_id=1, source_target_pairs={{0,3},{3,0},{1,2},{2,1},{4,7},{7,4},{5,6},{6,5},{8,11},{11,8},{9,1... | collective-permute-start | bytes 294920 | tf_op jit(solution)/shard_map/ppermute | solution.py:248
  78.6 8.1 %collective-permute-start.8 = (f32[16,128]{1,0:T(8,128)S(1)}, f32[16,128]{1,0:T(8,128)S(1)}, u32[]{:S(2)}, u32[]{:S(2)}) collective-permute-start(f32[16,128]{1,0:T(8,128)S(1)} %shard_map.69.refs_0_), channel_id=1, source_target_pairs={{0,3},{3,0},{1,2},{2,1},{4,7},{7,4},{5,6},{6,5},{8,11},{11,8},{9,1... | collective-permute-start | bytes 24584 | tf_op jit(solution)/shard_map/ppermute | solution.py:280
  85.4 4.0 %collective-permute-start.7 = (f32[16,128]{1,0:T(8,128)S(1)}, f32[16,128]{1,0:T(8,128)S(1)}, u32[]{:S(2)}, u32[]{:S(2)}) collective-permute-start(f32[16,128]{1,0:T(8,128)S(1)} %shard_map.69.refs_0_), channel_id=1, source_target_pairs={{0,2},{1,3},{2,0},{3,1},{4,6},{5,7},{6,4},{7,5},{8,10},{9,11},{10,... | collective-permute-start | bytes 24584 | tf_op jit(solution)/shard_map/ppermute | solution.py:281
  85.9 3.5 %collective-permute-start.6 = (f32[16,128]{1,0:T(8,128)S(1)}, f32[16,128]{1,0:T(8,128)S(1)}, u32[]{:S(2)}, u32[]{:S(2)}) collective-permute-start(f32[16,128]{1,0:T(8,128)S(1)} %shard_map.69.refs_0_), channel_id=1, source_target_pairs={{0,1},{1,0},{2,3},{3,2},{4,5},{5,4},{6,7},{7,6},{8,9},{9,8},{10,11... | collective-permute-start | bytes 24584 | tf_op jit(solution)/shard_map/ppermute | solution.py:282

commit v4 on v3

--- a/solution.py
+++ b/solution.py
@@ -169,22 +169,23 @@
     return lead, (value - lead.astype(jnp.float32)).astype(jnp.bfloat16)
 
 
-def gram_kernel(per_chunk, *refs):
-    recv_refs, out_ref, held = refs[:-7], refs[-7], refs[-6:]
+def gram_kernel(bands, odd_ref, recv_ref, own_ref, other_ref, *held):
     size = held[0].shape[0]
-    bands = per_chunk * len(recv_refs)
-    groups = size // bands
+    groups, part_size = size // bands, size // 2
+    odd = odd_ref[0]
     for f in range(2):
         for k in range(3):
             for band in range(bands):
-                ref = recv_refs[band // per_chunk]
-                first = ((band % per_chunk) * 2 + f) * 3 + k
-                part = ref[pl.ds(first, groups, stride=6 * per_chunk), :]
-                held[f * 3 + k][pl.ds(band, groups, stride=bands), :] = part
-    filt, image = (
-        terms(jnp.concatenate([ref[...] for ref in refs], axis=1)) for refs in (held[:3], held[3:])
+                part = recv_ref[pl.ds((band * 2 + f) * 3 + k, groups, stride=6 * bands), :]
+                if f == 0:
+                    held[k][pl.ds(band, groups, stride=bands), :] = part
+                other = odd if band < 2 else 1 - odd
+                rows = pl.ds(other * part_size + band % 2, groups, stride=2)
+                held[3 + f * 3 + k][rows, :] = part
+    right, filt, image = (
+        terms(jnp.concatenate([ref[...] for ref in held[i : i + 3]], axis=1)) for i in (0, 3, 6)
     )
-    right = jnp.concatenate([filt[0], filt[1], filt[0]], axis=1)
+    right = jnp.concatenate([right[0], right[1], right[0]], axis=1)
     for f, (lead, rest) in enumerate((filt, image)):
         block = lax.dot_general(
             jnp.concatenate([lead, lead, rest], axis=1),
@@ -193,22 +194,27 @@
             preferred_element_type=jnp.float32,
         )
         for c in range(2):
-            out_ref[pl.ds(f * 2 + c, size, stride=4), :] = block[:, c * 128 : (c + 1) * 128]
+            for i, ref in enumerate((own_ref, other_ref)):
+                piece = block[i * part_size : (i + 1) * part_size, c * 128 : (c + 1) * 128]
+                ref[pl.ds(f * 2 + c, part_size, stride=4), :] = piece
 
 
 def collect_kernel(recv_ref, out_ref):
     out_ref[...] = jnp.sum(recv_ref[...], axis=0)
 
 
-def finish_kernel(volume, own_ref, near_ref, over_ref, far_ref, corr_ref, proj_ref):
-    total = (own_ref[...] + over_ref[...]) + (near_ref[...] + far_ref[...])
-    total = total * volume
-    for band in range(corr_ref.shape[0]):
-        for c in range(2):
-            lanes = slice(c * 128, (c + 1) * 128)
-            row = band * 4 + c
-            corr_ref[band : band + 1, lanes] = total[row : row + 1]
-            proj_ref[band : band + 1, lanes] = total[row + 2 : row + 3]
+def finish_kernel(volume, odd_ref, own_ref, near_ref, over_ref, far_ref, corr_ref, proj_ref):
+    odd = odd_ref[0]
+    mine = (own_ref[...] + over_ref[...]) * volume
+    theirs = (near_ref[...] + far_ref[...]) * volume
+    for part in range(2):
+        total = jnp.where(odd == part, mine, theirs)
+        for line in range(2):
+            for c in range(2):
+                lanes = slice(c * 128, (c + 1) * 128)
+                row, band = line * 4 + c, part * 2 + line
+                corr_ref[band : band + 1, lanes] = total[row : row + 1]
+                proj_ref[band : band + 1, lanes] = total[row + 2 : row + 3]
 
 
 def shape(*dims):
@@ -270,20 +276,24 @@
     received = swapped.reshape(rows, nx)
 
     size = groups * count
-    parts = call(
-        lambda *refs: gram_kernel(count, *refs), shape(size * 4, 128), [(size, nx)] * 6
-    )(received)
-
-    swapped = lax.all_to_all(parts.reshape(groups, count * 4, 128), ("z", "y", "x"), 0, 0)
-    own = call(collect_kernel, shape(count * 4, 128))(swapped)
+    halves = shape(size * 2, 128)
+    mine, theirs = call(
+        lambda *refs: gram_kernel(count, *refs), (halves, halves), [(size, nx)] * 9, scalars=1
+    )(odd, received)
+    parts = mine + lax.ppermute(theirs, "slab", near)
+
+    swapped = lax.all_to_all(parts.reshape(groups, count * 2, 128), ("z", "y", "x"), 0, 0)
+    own = call(collect_kernel, shape(count * 2, 128))(swapped)
     over = [(i, (i + 2) % slabs) for i in range(slabs)]
     distant = lax.ppermute(own, "slab", far)
     opposite = lax.ppermute(own, "slab", over)
     sibling = lax.ppermute(own, "slab", near)
     volume = 1.0 / (slabs * thick * ny * nx)
     correlation, projected = call(
-        lambda *refs: finish_kernel(volume, *refs), (shape(count, 2 * 128), shape(count, 2 * 128))
-    )(own, sibling, opposite, distant)
+        lambda *refs: finish_kernel(volume, *refs),
+        (shape(count, 2 * 128), shape(count, 2 * 128)),
+        scalars=1,
+    )(odd, own, sibling, opposite, distant)
     return filtered, correlation, projected
 
 

time: 90.2 us -> 87.6 us (0.971)
  blocking collectives: 54.4 us -> 49.3 us
  starting transfers between devices: 18.3 us -> 19.6 us
  waiting for transfers between devices: 10.3 us -> 11.4 us
    all_to_all x1, blocking collectives: 21.9 us -> 16.8 us  [work(): lax.all_to_all(parts.reshape(groups, count * 2, 128), ('z', 'y', 'x'), 0, 0)]
    ppermute x0 -> x1, starting transfers between devices: none -> 2.89 us  [work(): parts = mine + lax.ppermute(theirs, 'slab', near)]
    ppermute x1, starting transfers between devices: 6.73 us -> 5.18 us  [work(): distant = lax.ppermute(own, 'slab', far)]
    ppermute x0 -> x1, waiting for transfers between devices: none -> 1.16 us  [work(): parts = mine + lax.ppermute(theirs, 'slab', near)]
  transfers between devices with their start and end apart: 9 -> 10, of which waited for: 4 -> 5; matrix products, arithmetic and copies ran while one was open for 0% -> 0% of each run, Pallas kernels for 0% -> 0%
where the time goes in v4:
time: 87.6 us; the launch traced here: 87.4 us
  blocking collectives  49.3 us (56%)
  starting transfers between devices  19.6 us (22%)
  waiting for transfers between devices  11.4 us (13%)
  Pallas kernels  5.23 us (6%)
  local copies, waits for them, and re-layouts  1.13 us (1%)
    all_to_all x1, blocking collectives, work(): lax.all_to_all(send.reshape(groups, -1, 2, nx), ('z', 'y', 'x'), 0, 0)  32.5 us
    all_to_all x1, blocking collectives, work(): lax.all_to_all(parts.reshape(groups, count * 2, 128), ('z', 'y', 'x'), 0, 0)  16.8 us
    pallas_call x4, Pallas kernels, run(): pl.pallas_call(kernel, out_shape=outs, in_specs=[pl.BlockSpec(memory_spac...  5.23 us
    ppermute x1, starting transfers between devices, work(): distant = lax.ppermute(own, 'slab', far)  5.18 us
    ppermute x1, waiting for transfers between devices, work(): pfar = lax.ppermute(potential, 'slab', far)  4.44 us
    ppermute x1, starting transfers between devices, work(): outer = lax.ppermute(paired[:, ::thick // 2 - 1], 'slab', far)  4.21 us
    ppermute x1, starting transfers between devices, work(): parts = mine + lax.ppermute(theirs, 'slab', near)  2.89 us
    ppermute x1, waiting for transfers between devices, work(): opposite = lax.ppermute(own, 'slab', over)  2.67 us
  transfers between devices with their start and end apart: 10, of which 5 were waited for; matrix products, arithmetic and copies ran while one was open for 0% of the time, Pallas kernels for 0%

profile of v4, /device:TPU:1, one launch (start us, length us, event | category | flops | bytes accessed | tf_op | source)
XLA Modules:
  0.0 87.4 jit_solution(17495243733548989932)
XLA Ops:
  0.6 0.0 copy-start
  0.6 0.0 copy-start.1
  0.6 0.0 copy-start.2
  0.7 0.0 copy-start.3
  0.7 1.1 %fusion = (f32[4,2,2,24,128]{4,3,2,1,0:T(8,128)S(1)}, f32[4,2,2,24,128]{4,3,2,1,0:T(8,128)S(1)}) fusion(f32[4,4,2,24,128]{4,3,2,1,0:T(8,128)} %bitcast.7), kind=kLoop, calls=%fused_computation.1 | loop fusion | bytes 786432 | tf_op jit(solution)/shard_map/slice | solution.py:257
  1.8 4.2 %collective-permute-start.1 = (f32[4,2,2,24,128]{4,3,2,1,0:T(8,128)S(1)}, f32[4,2,2,24,128]{4,3,2,1,0:T(8,128)S(1)}, u32[]{:S(2)}, u32[]{:S(2)}) collective-permute-start(f32[4,2,2,24,128]{4,3,2,1,0:T(8,128)S(1)} %get-tuple-element.16), channel_id=1, source_target_pairs={{0,3},{3,0},{1,2},{2,1},{4,7},{7,4},{5,6},{6,5},{8,11},{11,8},{9,1... | collective-permute-start | bytes 589832 | tf_op jit(solution)/shard_map/ppermute | solution.py:256
  6.0 0.0 copy-done
  6.0 0.0 collective-permute-start
  6.0 2.3 %collective-permute-start.2 = (f32[4,2,2,24,128]{4,3,2,1,0:T(8,128)S(1)}, f32[4,2,2,24,128]{4,3,2,1,0:T(8,128)S(1)}, u32[]{:S(2)}, u32[]{:S(2)}) collective-permute-start(f32[4,2,2,24,128]{4,3,2,1,0:T(8,128)S(1)} %get-tuple-element.15), channel_id=1, source_target_pairs={{0,3},{3,0},{1,2},{2,1},{4,7},{7,4},{5,6},{6,5},{8,11},{11,8},{9,1... | collective-permute-start | bytes 589832 | tf_op jit(solution)/shard_map/ppermute | solution.py:257
  8.3 2.4 %collective-permute-done.1.outer_ref = f32[4,2,2,24,128]{4,3,2,1,0:T(8,128)S(1)} collective-permute-done((f32[4,2,2,24,128]{4,3,2,1,0:T(8,128)S(1)}, f32[4,2,2,24,128]{4,3,2,1,0:T(8,128)S(1)}, u32[]{:S(2)}, u32[]{:S(2)}) %collective-permute-start.1) | collective-permute-done | bytes 196640 | tf_op jit(solution)/shard_map/ppermute | solution.py:256
  10.7 2.4 %collective-permute-start.3 = (f32[4,2,2,24,128]{4,3,2,1,0:T(8,128)S(1)}, f32[4,2,2,24,128]{4,3,2,1,0:T(8,128)S(1)}, u32[]{:S(2)}, u32[]{:S(2)}) collective-permute-start(f32[4,2,2,24,128]{4,3,2,1,0:T(8,128)S(1)} %collective-permute-done.1.outer_ref), channel_id=1, source_target_pairs={{0,1},{1,0},{2,3},{3,2},{4,5},{5,4},{6,7},{7,6},{8,9},{9,8},{10,11... | collective-permute-start | bytes 589832 | tf_op jit(solution)/shard_map/ppermute | solution.py:260
  13.1 0.0 collective-permute-start.4
  13.1 2.1 %collective-permute-start.5 = (f32[8,24,128]{2,1,0:T(8,128)S(1)}, f32[8,24,128]{2,1,0:T(8,128)S(1)}, u32[]{:S(2)}, u32[]{:S(2)}) collective-permute-start(f32[8,24,128]{2,1,0:T(8,128)S(1)} %copy-done.1), channel_id=1, source_target_pairs={{0,3},{3,0},{1,2},{2,1},{4,7},{7,4},{5,6},{6,5},{8,11},{11,8},{9,1... | collective-permute-start | bytes 294920 | tf_op jit(solution)/shard_map/ppermute | solution.py:254
  15.2 0.0 collective-permute-done.4.rest_0_
  15.2 4.4 %collective-permute-done.5.rest_2_ = f32[8,24,128]{2,1,0:T(8,128)S(1)} collective-permute-done((f32[8,24,128]{2,1,0:T(8,128)S(1)}, f32[8,24,128]{2,1,0:T(8,128)S(1)}, u32[]{:S(2)}, u32[]{:S(2)}) %collective-permute-start.5) | collective-permute-done | bytes 98336 | tf_op jit(solution)/shard_map/ppermute | solution.py:254
  19.6 0.0 collective-permute-done.2.inner_ref
  19.6 0.0 collective-permute-done.3.ends_ref
  19.6 0.0 collective-permute-done.near_ref
  19.7 3.9 %shard_map.67 = (f32[4,8,24,128]{3,2,1,0:T(8,128)}, f32[1536,128]{1,0:T(8,128)S(1)}) custom-call(s32[1]{0:T(128)} %bitcast.odd_ref.refs_0_, bf16[144,256]{1,0:T(8,128)(2,1)S(1)} %copy-done.2, bf16[256,128]{1,0:T(8,128)(2,1)S(1)} %copy-done.3, f32[4,8,24,128]{3,2,1,0:T(8,128)S(1)} %collective-permute-done.near_ref, f32[4,8,24,128]{3,2,1,0:T(8,128)S(1)} %copy-done, ...), custom_call_target="tpu_custom_call" | custom-call | tf_op jit(solution)/shard_map/pallas_call | solution.py:233
  23.6 32.5 %all_to_all.10 = f32[64,12,2,128]{3,2,1,0:T(2,128)S(1)} all-to-all(f32[64,12,2,128]{3,2,1,0:T(2,128)S(1)} %bitcast.8), channel_id=1, replica_groups=mesh['z'=8,'y'=4,'x'=2,'slab'=4] {'z','y','x'}, dimensions={0} | all-to-all | bytes 1572864 | tf_op jit(solution)/shard_map/all_to_all | solution.py:275
  56.1 0.6 shard_map.68
  56.7 2.9 %collective-permute-start.6 = (f32[512,128]{1,0:T(8,128)S(1)}, f32[512,128]{1,0:T(8,128)S(1)}, u32[]{:S(2)}, u32[]{:S(2)}) collective-permute-start(f32[512,128]{1,0:T(8,128)S(1)} %get-tuple-element.12), channel_id=1, source_target_pairs={{0,1},{1,0},{2,3},{3,2},{4,5},{5,4},{6,7},{7,6},{8,9},{9,8},{10,11... | collective-permute-start | bytes 786440 | tf_op jit(solution)/shard_map/ppermute | solution.py:283
  59.6 1.2 %collective-permute-done.6 = f32[512,128]{1,0:T(8,128)S(1)} collective-permute-done((f32[512,128]{1,0:T(8,128)S(1)}, f32[512,128]{1,0:T(8,128)S(1)}, u32[]{:S(2)}, u32[]{:S(2)}) %collective-permute-start.6) | collective-permute-done | bytes 262176 | tf_op jit(solution)/shard_map/ppermute | solution.py:283
  60.8 16.8 %all_to_all.11.recv_ref = f32[64,8,128]{2,1,0:T(8,128)S(1)} all-to-all(f32[64,8,128]{2,1,0:T(8,128)S(1)} %add_bitcast_fusion), channel_id=1, replica_groups=mesh['z'=8,'y'=4,'x'=2,'slab'=4] {'z','y','x'}, dimensions={0} | all-to-all | bytes 524288 | tf_op jit(solution)/shard_map/all_to_all | solution.py:285
  77.6 0.1 shard_map.69.refs_1_
  77.7 5.2 %collective-permute-start.9 = (f32[8,128]{1,0:T(8,128)S(1)}, f32[8,128]{1,0:T(8,128)S(1)}, u32[]{:S(2)}, u32[]{:S(2)}) collective-permute-start(f32[8,128]{1,0:T(8,128)S(1)} %shard_map.69.refs_1_), channel_id=1, source_target_pairs={{0,3},{3,0},{1,2},{2,1},{4,7},{7,4},{5,6},{6,5},{8,11},{11,8},{9,1... | collective-permute-start | bytes 12296 | tf_op jit(solution)/shard_map/ppermute | solution.py:288
  82.9 0.5 collective-permute-start.8
  83.4 0.0 collective-permute-start.7
  83.4 0.8 collective-permute-done.9.refs_4_
  84.2 2.7 %collective-permute-done.8.refs_3_ = f32[8,128]{1,0:T(8,128)S(1)} collective-permute-done((f32[8,128]{1,0:T(8,128)S(1)}, f32[8,128]{1,0:T(8,128)S(1)}, u32[]{:S(2)}, u32[]{:S(2)}) %collective-permute-start.8) | collective-permute-done | bytes 4128 | tf_op jit(solution)/shard_map/ppermute | solution.py:289
  86.8 0.0 collective-permute-done.7.refs_2_
  86.8 0.6 shard_map.70
  (4 shorter events, 0.0 us)
Async XLA Ops:
  0.6 5.4 %copy-start = (f32[4,8,24,128]{3,2,1,0:T(8,128)S(1)}, f32[4,8,24,128]{3,2,1,0:T(8,128)}, u32[]{:S(2)}) copy-start(f32[4,8,24,128]{3,2,1,0:T(8,128)} %mid_ref.1) | copy-start | bytes 1179652
  0.6 12.5 %copy-start.1 = (f32[8,24,128]{2,1,0:T(8,128)S(1)}, f32[8,24,128]{2,1,0:T(8,128)}, u32[]{:S(2)}) copy-start(f32[8,24,128]{2,1,0:T(8,128)} %rest_1_.1) | copy-start | bytes 294916
  0.6 19.0 %copy-start.2 = (bf16[144,256]{1,0:T(8,128)(2,1)S(1)}, bf16[144,256]{1,0:T(8,128)(2,1)}, u32[]{:S(2)}) copy-start(bf16[144,256]{1,0:T(8,128)(2,1)} %constant.21.clone.yz_ref) | copy-start | bytes 221188
  0.7 19.0 %copy-start.3 = (bf16[256,128]{1,0:T(8,128)(2,1)S(1)}, bf16[256,128]{1,0:T(8,128)(2,1)}, u32[]{:S(2)}) copy-start(bf16[256,128]{1,0:T(8,128)(2,1)} %constant.22.clone.x_ref) | copy-start | bytes 196612
  1.8 8.9 %collective-permute-start.1 = (f32[4,2,2,24,128]{4,3,2,1,0:T(8,128)S(1)}, f32[4,2,2,24,128]{4,3,2,1,0:T(8,128)S(1)}, u32[]{:S(2)}, u32[]{:S(2)}) collective-permute-start(f32[4,2,2,24,128]{4,3,2,1,0:T(8,128)S(1)} %get-tuple-element.16), channel_id=1, source_target_pairs={{0,3},{3,0},{1,2},{2,1},{4,7},{7,4},{5,6},{6,5},{8,11},{11,8},{9,1... | collective-permute-start | bytes 589832 | tf_op jit(solution)/shard_map/ppermute | solution.py:256
  6.0 13.7 %collective-permute-start = (f32[4,8,24,128]{3,2,1,0:T(8,128)S(1)}, f32[4,8,24,128]{3,2,1,0:T(8,128)S(1)}, u32[]{:S(2)}, u32[]{:S(2)}) collective-permute-start(f32[4,8,24,128]{3,2,1,0:T(8,128)S(1)} %copy-done), channel_id=1, source_target_pairs={{0,1},{1,0},{2,3},{3,2},{4,5},{5,4},{6,7},{7,6},{8,9},{9,8},{10,11... | collective-permute-start | bytes 1179656 | tf_op jit(solution)/shard_map/ppermute | solution.py:258
  6.0 13.6 %collective-permute-start.2 = (f32[4,2,2,24,128]{4,3,2,1,0:T(8,128)S(1)}, f32[4,2,2,24,128]{4,3,2,1,0:T(8,128)S(1)}, u32[]{:S(2)}, u32[]{:S(2)}) collective-permute-start(f32[4,2,2,24,128]{4,3,2,1,0:T(8,128)S(1)} %get-tuple-element.15), channel_id=1, source_target_pairs={{0,3},{3,0},{1,2},{2,1},{4,7},{7,4},{5,6},{6,5},{8,11},{11,8},{9,1... | collective-permute-start | bytes 589832 | tf_op jit(solution)/shard_map/ppermute | solution.py:257
  10.7 8.9 %collective-permute-start.3 = (f32[4,2,2,24,128]{4,3,2,1,0:T(8,128)S(1)}, f32[4,2,2,24,128]{4,3,2,1,0:T(8,128)S(1)}, u32[]{:S(2)}, u32[]{:S(2)}) collective-permute-start(f32[4,2,2,24,128]{4,3,2,1,0:T(8,128)S(1)} %collective-permute-done.1.outer_ref), channel_id=1, source_target_pairs={{0,1},{1,0},{2,3},{3,2},{4,5},{5,4},{6,7},{7,6},{8,9},{9,8},{10,11... | collective-permute-start | bytes 589832 | tf_op jit(solution)/shard_map/ppermute | solution.py:260
  13.1 2.1 %collective-permute-start.4 = (f32[8,24,128]{2,1,0:T(8,128)S(1)}, f32[8,24,128]{2,1,0:T(8,128)S(1)}, u32[]{:S(2)}, u32[]{:S(2)}) collective-permute-start(f32[8,24,128]{2,1,0:T(8,128)S(1)} %copy-done.1), channel_id=1, source_target_pairs={{0,1},{1,0},{2,3},{3,2},{4,5},{5,4},{6,7},{7,6},{8,9},{9,8},{10,11... | collective-permute-start | bytes 294920 | tf_op jit(solution)/shard_map/ppermute | solution.py:259
  13.1 6.5 %collective-permute-start.5 = (f32[8,24,128]{2,1,0:T(8,128)S(1)}, f32[8,24,128]{2,1,0:T(8,128)S(1)}, u32[]{:S(2)}, u32[]{:S(2)}) collective-permute-start(f32[8,24,128]{2,1,0:T(8,128)S(1)} %copy-done.1), channel_id=1, source_target_pairs={{0,3},{3,0},{1,2},{2,1},{4,7},{7,4},{5,6},{6,5},{8,11},{11,8},{9,1... | collective-permute-start | bytes 294920 | tf_op jit(solution)/shard_map/ppermute | solution.py:254
  56.7 4.0 %collective-permute-start.6 = (f32[512,128]{1,0:T(8,128)S(1)}, f32[512,128]{1,0:T(8,128)S(1)}, u32[]{:S(2)}, u32[]{:S(2)}) collective-permute-start(f32[512,128]{1,0:T(8,128)S(1)} %get-tuple-element.12), channel_id=1, source_target_pairs={{0,1},{1,0},{2,3},{3,2},{4,5},{5,4},{6,7},{7,6},{8,9},{9,8},{10,11... | collective-permute-start | bytes 786440 | tf_op jit(solution)/shard_map/ppermute | solution.py:283
  77.7 6.5 %collective-permute-start.9 = (f32[8,128]{1,0:T(8,128)S(1)}, f32[8,128]{1,0:T(8,128)S(1)}, u32[]{:S(2)}, u32[]{:S(2)}) collective-permute-start(f32[8,128]{1,0:T(8,128)S(1)} %shard_map.69.refs_1_), channel_id=1, source_target_pairs={{0,3},{3,0},{1,2},{2,1},{4,7},{7,4},{5,6},{6,5},{8,11},{11,8},{9,1... | collective-permute-start | bytes 12296 | tf_op jit(solution)/shard_map/ppermute | solution.py:288
  82.9 4.0 %collective-permute-start.8 = (f32[8,128]{1,0:T(8,128)S(1)}, f32[8,128]{1,0:T(8,128)S(1)}, u32[]{:S(2)}, u32[]{:S(2)}) collective-permute-start(f32[8,128]{1,0:T(8,128)S(1)} %shard_map.69.refs_1_), channel_id=1, source_target_pairs={{0,2},{1,3},{2,0},{3,1},{4,6},{5,7},{6,4},{7,5},{8,10},{9,11},{10,... | collective-permute-start | bytes 12296 | tf_op jit(solution)/shard_map/ppermute | solution.py:289
  83.4 3.4 %collective-permute-start.7 = (f32[8,128]{1,0:T(8,128)S(1)}, f32[8,128]{1,0:T(8,128)S(1)}, u32[]{:S(2)}, u32[]{:S(2)}) collective-permute-start(f32[8,128]{1,0:T(8,128)S(1)} %shard_map.69.refs_1_), channel_id=1, source_target_pairs={{0,1},{1,0},{2,3},{3,2},{4,5},{5,4},{6,7},{7,6},{8,9},{9,8},{10,11... | collective-permute-start | bytes 12296 | tf_op jit(solution)/shard_map/ppermute | solution.py:290

commit v5 on v4

--- a/solution.py
+++ b/solution.py
@@ -103,11 +103,12 @@
         near = dot(weights, split_ref[source, 0, window, :])
         near = near + dot(weights, split_ref[source, 1, window, :])
         lead, rest = split_ref[source, 0, here, :], split_ref[source, 1, here, :]
-        along = [
-            dot(jnp.concatenate([lead[:, lanes], rest[:, lanes]], axis=1), x_ref[...])
+        halves = [
+            jnp.concatenate([lead[:, lanes], rest[:, lanes]], axis=1)
             for lanes in (slice(0, nx), slice(nx, 2 * nx))
         ]
-        near = near + jnp.concatenate(along, axis=1)
+        along = dot(jnp.concatenate(halves, axis=0), x_ref[...])
+        near = near + jnp.concatenate([along[: planes * ny], along[planes * ny :]], axis=1)
         value = field_ref[level, here, :]
         weight = weight_ref[here, :]
         weight = jnp.concatenate([weight, weight], axis=1)
@@ -254,7 +255,8 @@
     pfar = lax.ppermute(potential, "slab", far)
     paired = bands.reshape(count, thick // 2, 2, ny, nx)
     outer = lax.ppermute(paired[:, :: thick // 2 - 1], "slab", far)
-    inner = lax.ppermute(paired[:, 1:-1], "slab", far)
+    middle = lax.optimization_barrier((paired, odd))[0][:, 1:-1]
+    inner = lax.ppermute(middle, "slab", far)
     beside = lax.ppermute(bands, "slab", near)
     pnear = lax.ppermute(potential, "slab", near)
     ends = lax.ppermute(outer, "slab", near)

time: 87.6 us -> 87.5 us (level)
  no operation moved by 1% of the time
where the time goes in v5:
time: 87.5 us; the launch traced here: 87.3 us
  blocking collectives  49.4 us (56%)
  starting transfers between devices  19.7 us (23%)
  waiting for transfers between devices  11.2 us (13%)
  Pallas kernels  5.26 us (6%)
  local copies, waits for them, and re-layouts  1.04 us (1%)
    all_to_all x1, blocking collectives, work(): lax.all_to_all(send.reshape(groups, -1, 2, nx), ('z', 'y', 'x'), 0, 0)  32.6 us
    all_to_all x1, blocking collectives, work(): lax.all_to_all(parts.reshape(groups, count * 2, 128), ('z', 'y', 'x'), 0, 0)  16.8 us
    pallas_call x4, Pallas kernels, run(): pl.pallas_call(kernel, out_shape=outs, in_specs=[pl.BlockSpec(memory_spac...  5.26 us
    ppermute x1, starting transfers between devices, work(): distant = lax.ppermute(own, 'slab', far)  5.2 us
    ppermute x1, waiting for transfers between devices, work(): pfar = lax.ppermute(potential, 'slab', far)  4.31 us
    ppermute x1, starting transfers between devices, work(): outer = lax.ppermute(paired[:, ::thick // 2 - 1], 'slab', far)  4.21 us
    ppermute x1, starting transfers between devices, work(): parts = mine + lax.ppermute(theirs, 'slab', near)  2.89 us
    ppermute x1, waiting for transfers between devices, work(): opposite = lax.ppermute(own, 'slab', over)  2.67 us
  transfers between devices with their start and end apart: 10, of which 5 were waited for; matrix products, arithmetic and copies ran while one was open for 0% of the time, Pallas kernels for 0%

profile of v5, /device:TPU:1, one launch (start us, length us, event | category | flops | bytes accessed | tf_op | source)
XLA Modules:
  0.0 87.3 jit_solution(6263100145097354780)
XLA Ops:
  0.6 0.0 copy-start
  0.6 1.0 %slice.6 = f32[4,2,2,24,128]{4,3,2,1,0:T(8,128)S(1)} slice(f32[4,4,2,24,128]{4,3,2,1,0:T(8,128)} %bitcast.7), slice={[0:4:1], [0:4:3], [0:2:1], [0:24:1], [0:128:1]} | slice | bytes 393216 | tf_op jit(solution)/shard_map/slice | solution.py:257
  1.6 4.2 %collective-permute-start.1 = (f32[4,2,2,24,128]{4,3,2,1,0:T(8,128)S(1)}, f32[4,2,2,24,128]{4,3,2,1,0:T(8,128)S(1)}, u32[]{:S(2)}, u32[]{:S(2)}) collective-permute-start(f32[4,2,2,24,128]{4,3,2,1,0:T(8,128)S(1)} %slice.6), channel_id=1, source_target_pairs={{0,3},{3,0},{1,2},{2,1},{4,7},{7,4},{5,6},{6,5},{8,11},{11,8},{9,1... | collective-permute-start | bytes 589832 | tf_op jit(solution)/shard_map/ppermute | solution.py:257
  5.9 0.0 copy-done
  5.9 0.0 collective-permute-start
  5.9 0.0 copy-start.3
  5.9 2.4 %collective-permute-start.2 = (f32[4,2,2,24,128]{4,3,2,1,0:T(8,128)S(1)}, f32[4,2,2,24,128]{4,3,2,1,0:T(8,128)S(1)}, u32[]{:S(2)}, u32[]{:S(2)}) collective-permute-start(f32[4,2,2,24,128]{4,3,2,1,0:T(8,128)S(1)} %slice.7), channel_id=1, source_target_pairs={{0,3},{3,0},{1,2},{2,1},{4,7},{7,4},{5,6},{6,5},{8,11},{11,8},{9,1... | collective-permute-start | bytes 589832 | tf_op jit(solution)/shard_map/ppermute | solution.py:259
  8.3 2.3 %collective-permute-done.1.outer_ref = f32[4,2,2,24,128]{4,3,2,1,0:T(8,128)S(1)} collective-permute-done((f32[4,2,2,24,128]{4,3,2,1,0:T(8,128)S(1)}, f32[4,2,2,24,128]{4,3,2,1,0:T(8,128)S(1)}, u32[]{:S(2)}, u32[]{:S(2)}) %collective-permute-start.1) | collective-permute-done | bytes 196640 | tf_op jit(solution)/shard_map/ppermute | solution.py:257
  10.6 2.3 %collective-permute-start.3 = (f32[4,2,2,24,128]{4,3,2,1,0:T(8,128)S(1)}, f32[4,2,2,24,128]{4,3,2,1,0:T(8,128)S(1)}, u32[]{:S(2)}, u32[]{:S(2)}) collective-permute-start(f32[4,2,2,24,128]{4,3,2,1,0:T(8,128)S(1)} %collective-permute-done.1.outer_ref), channel_id=1, source_target_pairs={{0,1},{1,0},{2,3},{3,2},{4,5},{5,4},{6,7},{7,6},{8,9},{9,8},{10,11... | collective-permute-start | bytes 589832 | tf_op jit(solution)/shard_map/ppermute | solution.py:262
  12.8 0.0 copy-done.1
  12.8 0.0 collective-permute-start.4
  12.8 2.2 %collective-permute-start.5 = (f32[8,24,128]{2,1,0:T(8,128)S(1)}, f32[8,24,128]{2,1,0:T(8,128)S(1)}, u32[]{:S(2)}, u32[]{:S(2)}) collective-permute-start(f32[8,24,128]{2,1,0:T(8,128)S(1)} %copy-done.1), channel_id=1, source_target_pairs={{0,3},{3,0},{1,2},{2,1},{4,7},{7,4},{5,6},{6,5},{8,11},{11,8},{9,1... | collective-permute-start | bytes 294920 | tf_op jit(solution)/shard_map/ppermute | solution.py:255
  15.1 0.0 collective-permute-done.4.rest_0_
  15.1 4.3 %collective-permute-done.5.rest_2_ = f32[8,24,128]{2,1,0:T(8,128)S(1)} collective-permute-done((f32[8,24,128]{2,1,0:T(8,128)S(1)}, f32[8,24,128]{2,1,0:T(8,128)S(1)}, u32[]{:S(2)}, u32[]{:S(2)}) %collective-permute-start.5) | collective-permute-done | bytes 98336 | tf_op jit(solution)/shard_map/ppermute | solution.py:255
  19.4 0.0 collective-permute-done.2.inner_ref
  19.4 0.0 collective-permute-done.3.ends_ref
  19.4 0.0 collective-permute-done.near_ref
  19.4 0.0 copy-done.2
  19.4 4.0 %shard_map.67 = (f32[4,8,24,128]{3,2,1,0:T(8,128)}, f32[1536,128]{1,0:T(8,128)S(1)}) custom-call(s32[1]{0:T(128)} %bitcast.odd_ref.refs_0_, bf16[144,256]{1,0:T(8,128)(2,1)S(1)} %copy-done.2, bf16[256,128]{1,0:T(8,128)(2,1)S(1)} %copy-done.3, f32[4,8,24,128]{3,2,1,0:T(8,128)S(1)} %collective-permute-done.near_ref, f32[4,8,24,128]{3,2,1,0:T(8,128)S(1)} %copy-done, ...), custom_call_target="tpu_custom_call" | custom-call | tf_op jit(solution)/shard_map/pallas_call | solution.py:234
  23.4 32.6 %all_to_all.10 = f32[64,12,2,128]{3,2,1,0:T(2,128)S(1)} all-to-all(f32[64,12,2,128]{3,2,1,0:T(2,128)S(1)} %bitcast.9), channel_id=1, replica_groups=mesh['z'=8,'y'=4,'x'=2,'slab'=4] {'z','y','x'}, dimensions={0} | all-to-all | bytes 1572864 | tf_op jit(solution)/shard_map/all_to_all | solution.py:277
  56.0 0.6 shard_map.68
  56.6 2.9 %collective-permute-start.6 = (f32[512,128]{1,0:T(8,128)S(1)}, f32[512,128]{1,0:T(8,128)S(1)}, u32[]{:S(2)}, u32[]{:S(2)}) collective-permute-start(f32[512,128]{1,0:T(8,128)S(1)} %get-tuple-element.14), channel_id=1, source_target_pairs={{0,1},{1,0},{2,3},{3,2},{4,5},{5,4},{6,7},{7,6},{8,9},{9,8},{10,11... | collective-permute-start | bytes 786440 | tf_op jit(solution)/shard_map/ppermute | solution.py:285
  59.5 1.2 %collective-permute-done.6 = f32[512,128]{1,0:T(8,128)S(1)} collective-permute-done((f32[512,128]{1,0:T(8,128)S(1)}, f32[512,128]{1,0:T(8,128)S(1)}, u32[]{:S(2)}, u32[]{:S(2)}) %collective-permute-start.6) | collective-permute-done | bytes 262176 | tf_op jit(solution)/shard_map/ppermute | solution.py:285
  60.7 16.8 %all_to_all.11.recv_ref = f32[64,8,128]{2,1,0:T(8,128)S(1)} all-to-all(f32[64,8,128]{2,1,0:T(8,128)S(1)} %add_bitcast_fusion), channel_id=1, replica_groups=mesh['z'=8,'y'=4,'x'=2,'slab'=4] {'z','y','x'}, dimensions={0} | all-to-all | bytes 524288 | tf_op jit(solution)/shard_map/all_to_all | solution.py:287
  77.5 0.1 shard_map.69.refs_1_
  77.6 5.2 %collective-permute-start.9 = (f32[8,128]{1,0:T(8,128)S(1)}, f32[8,128]{1,0:T(8,128)S(1)}, u32[]{:S(2)}, u32[]{:S(2)}) collective-permute-start(f32[8,128]{1,0:T(8,128)S(1)} %shard_map.69.refs_1_), channel_id=1, source_target_pairs={{0,3},{3,0},{1,2},{2,1},{4,7},{7,4},{5,6},{6,5},{8,11},{11,8},{9,1... | collective-permute-start | bytes 12296 | tf_op jit(solution)/shard_map/ppermute | solution.py:290
  82.8 0.5 collective-permute-start.8
  83.3 0.0 collective-permute-start.7
  83.3 0.8 collective-permute-done.9.refs_4_
  84.1 2.7 %collective-permute-done.8.refs_3_ = f32[8,128]{1,0:T(8,128)S(1)} collective-permute-done((f32[8,128]{1,0:T(8,128)S(1)}, f32[8,128]{1,0:T(8,128)S(1)}, u32[]{:S(2)}, u32[]{:S(2)}) %collective-permute-start.8) | collective-permute-done | bytes 4128 | tf_op jit(solution)/shard_map/ppermute | solution.py:291
  86.7 0.0 collective-permute-done.7.refs_2_
  86.7 0.6 shard_map.70
  (5 shorter events, 0.0 us)
Async XLA Ops:
  0.6 5.2 %copy-start = (f32[4,8,24,128]{3,2,1,0:T(8,128)S(1)}, f32[4,8,24,128]{3,2,1,0:T(8,128)}, u32[]{:S(2)}) copy-start(f32[4,8,24,128]{3,2,1,0:T(8,128)} %mid_ref.1) | copy-start | bytes 1179652
  1.6 8.9 %collective-permute-start.1 = (f32[4,2,2,24,128]{4,3,2,1,0:T(8,128)S(1)}, f32[4,2,2,24,128]{4,3,2,1,0:T(8,128)S(1)}, u32[]{:S(2)}, u32[]{:S(2)}) collective-permute-start(f32[4,2,2,24,128]{4,3,2,1,0:T(8,128)S(1)} %slice.6), channel_id=1, source_target_pairs={{0,3},{3,0},{1,2},{2,1},{4,7},{7,4},{5,6},{6,5},{8,11},{11,8},{9,1... | collective-permute-start | bytes 589832 | tf_op jit(solution)/shard_map/ppermute | solution.py:257
  5.9 13.5 %collective-permute-start = (f32[4,8,24,128]{3,2,1,0:T(8,128)S(1)}, f32[4,8,24,128]{3,2,1,0:T(8,128)S(1)}, u32[]{:S(2)}, u32[]{:S(2)}) collective-permute-start(f32[4,8,24,128]{3,2,1,0:T(8,128)S(1)} %copy-done), channel_id=1, source_target_pairs={{0,1},{1,0},{2,3},{3,2},{4,5},{5,4},{6,7},{7,6},{8,9},{9,8},{10,11... | collective-permute-start | bytes 1179656 | tf_op jit(solution)/shard_map/ppermute | solution.py:260
  5.9 7.0 %copy-start.1 = (f32[8,24,128]{2,1,0:T(8,128)S(1)}, f32[8,24,128]{2,1,0:T(8,128)}, u32[]{:S(2)}) copy-start(f32[8,24,128]{2,1,0:T(8,128)} %rest_1_.1) | copy-start | bytes 294916
  5.9 13.5 %copy-start.2 = (bf16[144,256]{1,0:T(8,128)(2,1)S(1)}, bf16[144,256]{1,0:T(8,128)(2,1)}, u32[]{:S(2)}) copy-start(bf16[144,256]{1,0:T(8,128)(2,1)} %constant.21.clone.yz_ref) | copy-start | bytes 221188
  5.9 13.5 %copy-start.3 = (bf16[256,128]{1,0:T(8,128)(2,1)S(1)}, bf16[256,128]{1,0:T(8,128)(2,1)}, u32[]{:S(2)}) copy-start(bf16[256,128]{1,0:T(8,128)(2,1)} %constant.22.clone.x_ref) | copy-start | bytes 196612
  5.9 13.5 %collective-permute-start.2 = (f32[4,2,2,24,128]{4,3,2,1,0:T(8,128)S(1)}, f32[4,2,2,24,128]{4,3,2,1,0:T(8,128)S(1)}, u32[]{:S(2)}, u32[]{:S(2)}) collective-permute-start(f32[4,2,2,24,128]{4,3,2,1,0:T(8,128)S(1)} %slice.7), channel_id=1, source_target_pairs={{0,3},{3,0},{1,2},{2,1},{4,7},{7,4},{5,6},{6,5},{8,11},{11,8},{9,1... | collective-permute-start | bytes 589832 | tf_op jit(solution)/shard_map/ppermute | solution.py:259
  10.6 8.8 %collective-permute-start.3 = (f32[4,2,2,24,128]{4,3,2,1,0:T(8,128)S(1)}, f32[4,2,2,24,128]{4,3,2,1,0:T(8,128)S(1)}, u32[]{:S(2)}, u32[]{:S(2)}) collective-permute-start(f32[4,2,2,24,128]{4,3,2,1,0:T(8,128)S(1)} %collective-permute-done.1.outer_ref), channel_id=1, source_target_pairs={{0,1},{1,0},{2,3},{3,2},{4,5},{5,4},{6,7},{7,6},{8,9},{9,8},{10,11... | collective-permute-start | bytes 589832 | tf_op jit(solution)/shard_map/ppermute | solution.py:262
  12.8 2.2 %collective-permute-start.4 = (f32[8,24,128]{2,1,0:T(8,128)S(1)}, f32[8,24,128]{2,1,0:T(8,128)S(1)}, u32[]{:S(2)}, u32[]{:S(2)}) collective-permute-start(f32[8,24,128]{2,1,0:T(8,128)S(1)} %copy-done.1), channel_id=1, source_target_pairs={{0,1},{1,0},{2,3},{3,2},{4,5},{5,4},{6,7},{7,6},{8,9},{9,8},{10,11... | collective-permute-start | bytes 294920 | tf_op jit(solution)/shard_map/ppermute | solution.py:261
  12.8 6.5 %collective-permute-start.5 = (f32[8,24,128]{2,1,0:T(8,128)S(1)}, f32[8,24,128]{2,1,0:T(8,128)S(1)}, u32[]{:S(2)}, u32[]{:S(2)}) collective-permute-start(f32[8,24,128]{2,1,0:T(8,128)S(1)} %copy-done.1), channel_id=1, source_target_pairs={{0,3},{3,0},{1,2},{2,1},{4,7},{7,4},{5,6},{6,5},{8,11},{11,8},{9,1... | collective-permute-start | bytes 294920 | tf_op jit(solution)/shard_map/ppermute | solution.py:255
  56.6 4.0 %collective-permute-start.6 = (f32[512,128]{1,0:T(8,128)S(1)}, f32[512,128]{1,0:T(8,128)S(1)}, u32[]{:S(2)}, u32[]{:S(2)}) collective-permute-start(f32[512,128]{1,0:T(8,128)S(1)} %get-tuple-element.14), channel_id=1, source_target_pairs={{0,1},{1,0},{2,3},{3,2},{4,5},{5,4},{6,7},{7,6},{8,9},{9,8},{10,11... | collective-permute-start | bytes 786440 | tf_op jit(solution)/shard_map/ppermute | solution.py:285
  77.6 6.5 %collective-permute-start.9 = (f32[8,128]{1,0:T(8,128)S(1)}, f32[8,128]{1,0:T(8,128)S(1)}, u32[]{:S(2)}, u32[]{:S(2)}) collective-permute-start(f32[8,128]{1,0:T(8,128)S(1)} %shard_map.69.refs_1_), channel_id=1, source_target_pairs={{0,3},{3,0},{1,2},{2,1},{4,7},{7,4},{5,6},{6,5},{8,11},{11,8},{9,1... | collective-permute-start | bytes 12296 | tf_op jit(solution)/shard_map/ppermute | solution.py:290
  82.8 4.0 %collective-permute-start.8 = (f32[8,128]{1,0:T(8,128)S(1)}, f32[8,128]{1,0:T(8,128)S(1)}, u32[]{:S(2)}, u32[]{:S(2)}) collective-permute-start(f32[8,128]{1,0:T(8,128)S(1)} %shard_map.69.refs_1_), channel_id=1, source_target_pairs={{0,2},{1,3},{2,0},{3,1},{4,6},{5,7},{6,4},{7,5},{8,10},{9,11},{10,... | collective-permute-start | bytes 12296 | tf_op jit(solution)/shard_map/ppermute | solution.py:291
  83.3 3.5 %collective-permute-start.7 = (f32[8,128]{1,0:T(8,128)S(1)}, f32[8,128]{1,0:T(8,128)S(1)}, u32[]{:S(2)}, u32[]{:S(2)}) collective-permute-start(f32[8,128]{1,0:T(8,128)S(1)} %shard_map.69.refs_1_), channel_id=1, source_target_pairs={{0,1},{1,0},{2,3},{3,2},{4,5},{5,4},{6,7},{7,6},{8,9},{9,8},{10,11... | collective-permute-start | bytes 12296 | tf_op jit(solution)/shard_map/ppermute | solution.py:292
